TPU v7x, 32 devices: a whole 2x2x4 slice. The times are simulated.
32 devices in a mesh: groups: 1, expert: 8 (over z, y), tensor: 2 (over x), pair: 2 (over core).
Axes of the slice: x: 2, y: 2, z: 4, core: 2. Of those that a mesh axis runs over, the one named last changes fastest.
Arguments:
- tokens: bfloat16 [512, 3584], P(('groups', 'expert', 'tensor', 'pair')), may hold values from -6 to 6
- expert_ids: int32 [512, 8], P(('groups', 'expert', 'tensor', 'pair')), may hold values from 0 to 15, all different within a row; in each aligned block of 16 rows (0 to 15, 16 to 31, ...) at most 16 rows name the same one
- route_weight: float32 [512, 8], P(('groups', 'expert', 'tensor', 'pair')), may hold values from 0.05 to 0.5
- w_gate: bfloat16 [16, 3584, 1024], P(('expert', 'pair'), None, 'tensor'), may hold values from -0.09375 to 0.09375
- w_up: bfloat16 [16, 3584, 1024], P(('expert', 'pair'), None, 'tensor'), may hold values from -0.09375 to 0.09375
- w_down: bfloat16 [16, 1024, 3584], P(('expert', 'pair'), 'tensor'), may hold values from -0.1875 to 0.1875
- s_gate: bfloat16 [3584, 2048], P(None, ('tensor', 'pair')), may hold values from -0.09375 to 0.09375
- s_up: bfloat16 [3584, 2048], P(None, ('tensor', 'pair')), may hold values from -0.09375 to 0.09375
- s_down: bfloat16 [2048, 3584], P(('tensor', 'pair')), may hold values from -0.125 to 0.125
Outputs:
- moe_out: bfloat16 [512, 3584], P(('groups', 'expert', 'tensor', 'pair'))
Inputs may be any that keep to these rules, and one draw needn't show every extreme that they name: `expert_ids`: each row names 8 different experts. Among the 16 tokens of one device no expert is named by more than 16 tokens, and in every draw some expert is named by exactly 16 tokens of some device.
All inputs are finite; a program needn't handle non-finite values.
Results may differ from a plain program's by a relative error of at most 0.014.
Values may be sent and summed in bfloat16 or wider, within the bound.
A program may use at most 64 MiB of HBM per device.

v0:
```python
import functools

import jax
import jax.numpy as jnp
from jax import lax
from jax.experimental import pallas as pl
from jax.experimental.pallas import tpu as pltpu
from jax.sharding import PartitionSpec as P

MESH = pl.DeviceIdType.MESH
F32 = jnp.float32
BF16 = jnp.bfloat16


def lanes_for(experts):
    return -(-3 * experts // 128) * 128


def tile_of(width, most):
    for tile in range(min(width, most), 0, -1):
        if width % tile == 0 and (tile % 128 == 0 or tile == width):
            return tile
    return width


class Layout:
    def __init__(self, n_expert, n_tensor, n_pair, tok_rows):
        self.n_expert, self.n_tensor, self.n_pair = n_expert, n_tensor, n_pair
        self.ny = 2 if n_expert % 2 == 0 else 1
        self.nz = n_expert // self.ny
        self.half = n_expert * n_tensor
        self.blocks = 2 * self.half
        self.rows = tok_rows
        self.first = (n_tensor, self.ny)
        self.last = (self.ny, n_tensor)

    def steps(self, z):
        out = [[(z, None)]]
        for k in range(1, self.nz):
            out.append([(z + k, z + k < self.nz), (z - k, z - k >= 0)])
        return out


def kernel(lay, experts, tok_in, ids_in, rw_in, wg_in, wu_in, wd_in, sg_in, su_in, sd_in, out,
           tok, part, ids, rw, recvp, recvb0, recvb1, recva0, recva1, recvz, xs, hid, hs,
           wg, wu, wd, sg, su, sd, load_sem, tok_send, tok_recv, red_send, red_recv):
    nz, ny, nt = lay.nz, lay.ny, lay.n_tensor
    rows, half = lay.rows, lay.half
    width = part.shape[-1]
    e_idx, t, p = lax.axis_index("expert"), lax.axis_index("tensor"), lax.axis_index("pair")
    z, y = e_idx // ny, e_idx % ny

    def device(z_, y_, t_):
        return {"expert": z_ * ny + y_, "tensor": t_, "pair": p}

    partner = {"expert": e_idx, "tensor": t, "pair": 1 - p}
    t_peers = [(t + d) % nt for d in range(1, nt)]
    y_peers = [(y + d) % ny for d in range(1, ny)]
    z_peers = [(z + d) % nz for d in range(1, nz)]

    def place(q, z_, y_, t_):
        return ((q * nz + z_) * ny + y_) * nt + t_

    cut = width // 256 * 128
    wide = (pl.ds(0, cut), pl.ds(cut, tok.shape[-1] - cut))
    cols2 = (pl.ds(0, cut), pl.ds(cut, width - cut))
    first_peers, last_peers = (t_peers, y_peers), (y_peers, t_peers)
    first_at, last_at = (t, y), (y, t)

    def yt(h, first_, last_):
        return (last_, first_) if h == 0 else (first_, last_)

    own = place(p, z, y, t)
    first = pltpu.make_async_copy(tok_in, tok.at[own, :, pl.ds(0, width)], load_sem.at[6])
    first.start()
    small = [pltpu.make_async_copy(ids_in, ids, load_sem.at[7]), pltpu.make_async_copy(rw_in, rw, load_sem.at[8])]
    for load in small:
        load.start()
    loads = [
        pltpu.make_async_copy(src, dst, load_sem.at[i])
        for i, (src, dst) in enumerate(
            ((sg_in, sg), (su_in, su), (sd_in, sd), (wg_in.at[0], wg), (wu_in.at[0], wu), (wd_in.at[0], wd))
        )
    ]
    for load in loads:
        load.start()

    barrier = pltpu.get_barrier_semaphore()

    def greet(dev):
        pl.semaphore_signal(barrier, inc=1, device_id=dev, device_id_type=MESH)

    greet(partner)
    for t_ in t_peers:
        greet(device(z, y, t_))
    for y_ in y_peers:
        greet(device(z, y_, t))
    for z_ in z_peers:
        greet(device(z_, y, t))

    for load in small:
        load.wait()
    lane = lax.broadcasted_iota(jnp.int32, (rows, tok.shape[-1] - width), 1)
    top = ids.shape[1]
    pieces = [jnp.zeros(lane.shape, F32) for _ in range(3)]
    for k in range(top):
        for m in range(3):
            pieces[m] = pieces[m] + jnp.where(lane == ids[:, k : k + 1] + m * experts, rw[:, k : k + 1], 0.0)
    hi = [v.astype(BF16).astype(F32) for v in pieces]
    rest = [v - h for v, h in zip(pieces, hi)]
    mid = [v.astype(BF16).astype(F32) for v in rest]
    low = [v - h for v, h in zip(rest, mid)]
    tok[own, :, pl.ds(width, lane.shape[1])] = (hi[0] + mid[1] + low[2]).astype(BF16)

    pl.semaphore_wait(barrier, nt + ny + nz - 2)

    first.wait()

    sent = []

    def both(c1, c2):
        return c2 if c1 is None else (c1 if c2 is None else jnp.logical_and(c1, c2))

    def run(cond, fn):
        if cond is None:
            fn()
        else:
            pl.when(cond)(fn)

    def send(src, dst, sem_send, sem_recv, dev, cond=None):
        copy = pltpu.make_async_remote_copy(
            src_ref=src, dst_ref=dst, send_sem=sem_send, recv_sem=sem_recv,
            device_id=dev, device_id_type=MESH)
        run(cond, copy.start)
        sent.append((cond, copy))

    counter = [0]

    def send_block(h, idx, dev, cond=None):
        view = tok.at[idx, :, wide[h]]
        send(view, view, tok_send.at[counter[0]], tok_recv.at[h, idx], dev, cond)
        counter[0] += 1

    def arrive(h, idx, cond=None):
        view = tok.at[idx, :, wide[h]]
        copy = pltpu.make_async_remote_copy(
            src_ref=view, dst_ref=view, send_sem=tok_send.at[0],
            recv_sem=tok_recv.at[h, idx], device_id=partner, device_id_type=MESH)
        run(cond, copy.wait_recv)

    def last_sends(h, idx, cond):
        for v in last_peers[h]:
            send_block(h, idx, device(z, *yt(h, first_at[h], v)), cond)

    def stage_line(k):
        for z_, cond in line[k]:
            blk = place(p, z_, y, t)
            for h in range(2):
                if k:
                    arrive(h, blk, cond)
                for v in first_peers[h]:
                    send_block(h, blk, device(z, *yt(h, v, last_at[h])), cond)
            for h in range(2):
                last_sends(h, blk, cond)
                send_block(h, blk, partner, cond)

    def stage_first(k):
        for z_, cond in line[k]:
            for d in range(max(ny, nt) - 1):
                for h in range(2):
                    if d < len(first_peers[h]):
                        blk = place(p, z_, *yt(h, first_peers[h][d], last_at[h]))
                        arrive(h, blk, cond)
                        last_sends(h, blk, cond)
                        send_block(h, blk, partner, cond)

    def stage_last(k):
        for z_, cond in line[k]:
            for h in range(2):
                for f in [first_at[h]] + first_peers[h]:
                    for v in last_peers[h]:
                        blk = place(p, z_, *yt(h, f, v))
                        arrive(h, blk, cond)
                        send_block(h, blk, partner, cond)

    line = lay.steps(z)
    for k in range(1, nz):
        for z_, cond in line[k]:
            for h in range(2):
                send_block(h, own, device(z_, y, t), cond)
    for k in range(nz + 2):
        if k < nz:
            stage_line(k)
        if 0 <= k - 1 < nz:
            stage_first(k - 1)
        if 0 <= k - 2 < nz:
            stage_last(k - 2)
    for k in range(nz):
        for z_, cond in line[k]:
            for y_ in range(ny):
                for t_ in range(nt):
                    for h in range(2):
                        arrive(h, place(1 - p, z_, y_, t_), cond)

    group = []
    for q in range(2):
        for t_ in range(lay.n_tensor):
            group.append(place(q, z, y, t_))
    for i, idx in enumerate(group):
        xs[i] = tok[idx, :, pl.ds(0, width)]
    count = len(group)

    def hidden_tiles(x, w1, w2, scale, store):
        tile = tile_of(w1.shape[1], 256)

        def body(n, _):
            cols = pl.ds(pl.multiple_of(n * tile, tile), tile)
            g = jnp.dot(x(), w1[:, cols], preferred_element_type=F32)
            u = jnp.dot(x(), w2[:, cols], preferred_element_type=F32)
            h = g / (1.0 + jnp.exp(-g)) * u
            if scale is not None:
                h = h * scale
            store[:, cols] = h.astype(BF16)
            return 0

        lax.fori_loop(0, w1.shape[1] // tile, body, 0)

    loads[0].wait()
    loads[1].wait()
    hidden_tiles(lambda: xs[...].reshape(count * rows, width), sg, su, None, hs)
    loads[2].wait()
    for i in range(3, 6):
        loads[i].wait()

    out_tile = tile_of(width, 512)
    per = min(half, max(1, 256 // rows))
    while half % per:
        per -= 1
    mine = e_idx * lay.n_pair + p

    def chunk(c, _):
        at = c * per
        extra = tok[pl.ds(at, per), :, pl.ds(width, lane.shape[1])].reshape(per * rows, lane.shape[1])
        l2 = lax.broadcasted_iota(jnp.int32, extra.shape, 1)
        pick = (l2 == mine) | (l2 == mine + experts) | (l2 == mine + 2 * experts)
        scale = jnp.sum(jnp.where(pick, extra.astype(F32), 0.0), axis=1, keepdims=True)
        hidden_tiles(lambda: tok[pl.ds(at, per), :, pl.ds(0, width)].reshape(per * rows, width), wg, wu, scale, hid)

        def body(n, _):
            cols = pl.ds(pl.multiple_of(n * out_tile, out_tile), out_tile)
            v = jnp.dot(hid[...], wd[:, cols], preferred_element_type=F32)
            part[pl.ds(at, per), :, cols] = v.astype(BF16).reshape(per, rows, out_tile)
            return 0

        lax.fori_loop(0, width // out_tile, body, 0)
        return 0

    def shared_into(q):
        lo = q * (count // 2)

        def body(n, _):
            cols = pl.ds(pl.multiple_of(n * out_tile, out_tile), out_tile)
            r0 = pl.multiple_of(lo * rows, rows)
            v = jnp.dot(hs[pl.ds(r0, count // 2 * rows), :], sd[:, cols], preferred_element_type=F32)
            for j in range(count // 2):
                idx = place(q, z, y, j)
                part[idx, :, cols] = (part[idx, :, cols].astype(F32) + v[j * rows : (j + 1) * rows]).astype(BF16)
            return 0

        lax.fori_loop(0, width // out_tile, body, 0)

    rcount = [0]

    def send_sum(src, dst, recv_at, dev, cond=None):
        send(src, dst, red_send.at[rcount[0]], red_recv.at[recv_at], dev, cond)
        rcount[0] += 1

    def got(dst, recv_at, cond=None):
        copy = pltpu.make_async_remote_copy(
            src_ref=dst, dst_ref=dst, send_sem=red_send.at[0], recv_sem=red_recv.at[recv_at],
            device_id=partner, device_id_type=MESH)
        run(cond, copy.wait_recv)

    steps = half // per
    other = 1 - p
    lax.fori_loop(0, steps, lambda c, v: chunk(other * steps + c, v), 0)
    shared_into(other)

    recvb, recva = (recvb0, recvb1), (recva0, recva1)
    base = [half]
    bases = {}

    def at(kind, h, n):
        if (kind, h) not in bases:
            bases[kind, h] = base[0]
            base[0] += n
        return bases[kind, h]

    far = [pair for k in range(nz - 1, -1, -1) for pair in line[k]]

    for y_ in range(ny):
        for z_ in range(nz):
            at_ = z_ * ny + y_
            send_sum(part.at[pl.ds(place(other, z_, y_, 0), nt)], recvp.at[pl.ds(at_ * nt, nt)], at_, partner)
    lax.fori_loop(0, steps, lambda c, v: chunk(p * steps + c, v), 0)
    shared_into(p)

    def buf_b(h, d, z_, f):
        n = lay.first[h]
        at_ = (d * nz + z_) * n + f
        return recvb[h].at[at_], at("b", h, (lay.last[h] - 1) * nz * n) + at_

    def buf_a(h, d, z_):
        return recva[h].at[d * nz + z_], at("a", h, (lay.first[h] - 1) * nz) + d * nz + z_

    def buf_z(h, d):
        return recvz.at[d, :, cols2[h]], at("z", h, nz - 1) + d

    def add_into(h, idx, others, cond):
        def fn():
            v = part[idx, :, cols2[h]].astype(F32)
            for ref in others:
                v = v + ref[...].astype(F32)
            part[idx, :, cols2[h]] = v.astype(BF16)
        run(cond, fn)

    def mine_of(z_, y_, t_, h):
        return recvp.at[(z_ * ny + y_) * nt + t_, :, cols2[h]]

    def sums_last(z_, cond):
        for y_ in [(y + 1 + d) % ny for d in range(ny)]:
            got(recvp.at[pl.ds((z_ * ny + y_) * nt, nt)], z_ * ny + y_, cond)
        for f in range(max(ny, nt) - 1, -1, -1):
            for h in range(2):
                firsts = [first_at[h]] + first_peers[h]
                if f >= len(firsts):
                    continue
                for d, v in enumerate(last_peers[h]):
                    y_, t_ = yt(h, firsts[f], v)
                    idx = place(p, z_, y_, t_)
                    add_into(h, idx, [mine_of(z_, y_, t_, h)], cond)
                    ref, sem = buf_b(h, d, z_, firsts[f])
                    y2, t2 = yt(h, first_at[h], v)
                    send_sum(part.at[idx, :, cols2[h]], ref, sem, device(z, y2, t2), cond)

    def collect_last(h, z_, f, cond):
        y_, t_ = yt(h, f, last_at[h])
        refs = [mine_of(z_, y_, t_, h)]
        for d in range(lay.last[h] - 1):
            ref, sem = buf_b(h, d, z_, f)
            got(ref, sem, cond)
            refs.append(ref)
        return place(p, z_, y_, t_), refs

    def sums_first(z_, cond):
        for h in range(2):
            for d, f in enumerate(first_peers[h]):
                idx, refs = collect_last(h, z_, f, cond)
                add_into(h, idx, refs, cond)
                ref, sem = buf_a(h, d, z_)
                send_sum(part.at[idx, :, cols2[h]], ref, sem, device(z, *yt(h, f, last_at[h])), cond)

    def sums_line(z_, cond):
        for h in range(2):
            idx, refs = collect_last(h, z_, first_at[h], cond)
            for d in range(lay.first[h] - 1):
                ref, sem = buf_a(h, d, z_)
                got(ref, sem, cond)
                refs.append(ref)
            if cond is None:
                for d in range(nz - 1):
                    ref, sem = buf_z(h, d)
                    got(ref, sem)
                    refs.append(ref)
            add_into(h, idx, refs, cond)
            if cond is not None:
                d = (z_ - z + nz) % nz - 1
                ref, sem = buf_z(h, d)
                send_sum(part.at[idx, :, cols2[h]], ref, sem, device(z_, y, t), cond)

    for i in range(len(far) + 4):
        if i < len(far):
            sums_last(*far[i])
        if 0 <= i - 2 < len(far):
            sums_first(*far[i - 2])
        if 0 <= i - 4 < len(far):
            sums_line(*far[i - 4])
    total = part[own]
    out[...] = total
    for cond, copy in sent:
        run(cond, copy.wait_send)


def per_device(lay, experts, tokens, ids, rw, wg, wu, wd, sg, su, sd):
    rows, width = tokens.shape
    nz, ny, nt = lay.nz, lay.ny, lay.n_tensor
    cut = width // 256 * 128
    count = 2 * lay.n_tensor
    hidden, shared = wg.shape[2], sg.shape[1]
    per = min(lay.half, max(1, 256 // rows))
    while lay.half % per:
        per -= 1
    span = 2 * nz - 1
    sends = 4 * (nz - 1) + span * (nt - 1 + ny - 1) + 2 * span * (nt * ny) + span * 2 * nt * ny
    red = nz * ny + 2 * span * nt * ny + 4 * nz + 2 * span * (nt + ny)
    halves = (cut, width - cut)
    many_b = [max(1, (lay.last[h] - 1) * nz * lay.first[h]) for h in range(2)]
    many_a = [max(1, (lay.first[h] - 1) * nz) for h in range(2)]
    vmem = pl.BlockSpec(memory_space=pltpu.VMEM)
    anyw = pl.BlockSpec(memory_space=pl.ANY)
    scratch = [
        pltpu.VMEM((lay.blocks, rows, width + lanes_for(experts)), BF16),
        pltpu.VMEM((lay.blocks, rows, width), BF16),
        pltpu.VMEM(ids.shape, jnp.int32),
        pltpu.VMEM(rw.shape, F32),
        pltpu.VMEM((lay.half, rows, width), BF16),
        pltpu.VMEM((many_b[0], rows, halves[0]), BF16),
        pltpu.VMEM((many_b[1], rows, halves[1]), BF16),
        pltpu.VMEM((many_a[0], rows, halves[0]), BF16),
        pltpu.VMEM((many_a[1], rows, halves[1]), BF16),
        pltpu.VMEM((max(1, nz - 1), rows, width), BF16),
        pltpu.VMEM((count, rows, width), BF16),
        pltpu.VMEM((per * rows, hidden), BF16),
        pltpu.VMEM((count * rows, shared), BF16),
        pltpu.VMEM(wg.shape[1:], BF16),
        pltpu.VMEM(wu.shape[1:], BF16),
        pltpu.VMEM(wd.shape[1:], BF16),
        pltpu.VMEM(sg.shape, BF16),
        pltpu.VMEM(su.shape, BF16),
        pltpu.VMEM(sd.shape, BF16),
        pltpu.SemaphoreType.DMA((9,)),
        pltpu.SemaphoreType.DMA((sends,)),
        pltpu.SemaphoreType.DMA((2, lay.blocks)),
        pltpu.SemaphoreType.DMA((red,)),
        pltpu.SemaphoreType.DMA((lay.half + sum(many_b) + sum(many_a) + 2 * nz,)),
    ]
    return pl.pallas_call(
        functools.partial(kernel, lay, experts),
        out_shape=jax.ShapeDtypeStruct((rows, width), BF16),
        in_specs=[anyw] * 9,
        out_specs=vmem,
        scratch_shapes=scratch,
        compiler_params=pltpu.CompilerParams(
            collective_id=0, has_side_effects=True, vmem_limit_bytes=67043328
        ),
    )(tokens, ids, rw, wg, wu, wd, sg, su, sd)


def solution(mesh):
    shape = dict(mesh.shape)

    def body(tokens, ids, rw, wg, wu, wd, sg, su, sd):
        lay = Layout(shape["expert"], shape["tensor"], shape["pair"], tokens.shape[0])
        experts = shape["expert"] * shape["pair"] * wg.shape[0]
        return per_device(lay, experts, tokens, ids, rw, wg, wu, wd, sg, su, sd)

    in_specs = (
        P(("groups", "expert", "tensor", "pair"), None),
        P(("groups", "expert", "tensor", "pair"), None),
        P(("groups", "expert", "tensor", "pair"), None),
        P(("expert", "pair"), None, "tensor"),
        P(("expert", "pair"), None, "tensor"),
        P(("expert", "pair"), "tensor", None),
        P(None, ("tensor", "pair")),
        P(None, ("tensor", "pair")),
        P(("tensor", "pair"), None),
    )
    out_specs = P(("groups", "expert", "tensor", "pair"), None)
    return jax.shard_map(body, mesh=mesh, in_specs=in_specs, out_specs=out_specs, check_vma=False)
```

profile of v0, /device:TPU:0, one launch (start us, length us, event | category | flops | bytes accessed | tf_op | source)
XLA Modules:
  0.0 68.3 jit_solution(8721064974502658171)
XLA Ops:
  0.0 1.4 %copy.10.ids_in = s32[16,8]{1,0:T(8,128)} copy(s32[16,8]{0,1:T(8,128)} %param.10) | data formatting | bytes 1024 | tf_op args[1]
  1.4 1.4 %copy.11.rw_in = f32[16,8]{1,0:T(8,128)} copy(f32[16,8]{0,1:T(8,128)} %param.11) | data formatting | bytes 1024 | tf_op args[2]
  2.7 64.1 %shard_map.91 = bf16[16,3584]{1,0:T(8,128)(2,1)} custom-call(bf16[16,3584]{1,0:T(8,128)(2,1)} %tok_in.1, s32[16,8]{1,0:T(8,128)} %copy.10.ids_in, f32[16,8]{1,0:T(8,128)} %copy.11.rw_in, bf16[1,3584,512]{2,1,0:T(8,128)(2,1)} %wg_in.1, bf16[1,3584,512]{2,1,0:T(8,128)(2,1)} %wu_in.1, bf16[1,512,3584]{2,1,0:T(8,128)(2,1)} %wd_in.1, bf16[3584,512]{1,0:T(8,128)(2,1)} %sg_in.1, ...), custom_call_target="tpu_custom_call" | custom-call | tf_op jit(solution)/shard_map/pallas_call | solution.py:437
  66.8 1.6 %copy.13 = bf16[16,3584]{1,0:T(8,128)(2,1)} copy(bf16[16,3584]{1,0:T(8,128)(2,1)} %shard_map.91) | data formatting | bytes 229376
where the time goes:
time: 68.6 us; the launch traced here: 68.3 us
  Pallas kernels  64.1 us (93%)
  local copies, waits for them, and re-layouts  4.26 us (6%)
    pallas_call x1, Pallas kernels, per_device(): pl.pallas_call(functools.partial(kernel, lay, experts), out_shape=jax.Sha...  64.1 us
    unnamed x3, local copies, waits for them, and re-layouts  4.26 us

commit v1 on v0

v1 whole, which is shorter than its diff:
```python
import functools

import jax
import jax.numpy as jnp
from jax import lax
from jax.experimental import pallas as pl
from jax.experimental.pallas import tpu as pltpu
from jax.sharding import PartitionSpec as P

MESH = pl.DeviceIdType.MESH
F32 = jnp.float32
BF16 = jnp.bfloat16


def lanes_for(experts):
    return -(-3 * experts // 128) * 128


def tile_of(width, most):
    for tile in range(min(width, most), 0, -1):
        if width % tile == 0 and (tile % 128 == 0 or tile == width):
            return tile
    return width


class Layout:
    def __init__(self, n_expert, n_tensor, tok_rows, width, experts):
        self.nt = n_tensor
        self.ny = 2 if n_expert % 2 == 0 else 1
        self.nz = n_expert // self.ny
        self.chips = self.ny * self.nt
        self.plane = 2 * self.chips
        self.blocks = self.nz * self.plane
        self.rows, self.width, self.extra = tok_rows, width, lanes_for(experts)
        cut = width // 256 * 128
        self.cols = [(0, cut), (cut, width - cut)]
        self.wide = [(0, cut), (cut, width - cut + self.extra)]
        self.first = (self.nt, self.ny)
        self.last = (self.ny, self.nt)

    def sequence(self, z):
        nz = self.nz
        m = jnp.minimum(z, nz - 1 - z)
        out = [z]
        for i in range(1, nz):
            near = z + (i + 1) // 2 if i % 2 else z - i // 2
            far = jnp.where(z <= nz - 1 - z, z + (i - m), z - (i - m))
            out.append(jnp.where(i <= 2 * m, near, far))
        return out


def schedule(nz):
    ops = [("A2", 0), ("A1", 1), ("A3", 0), ("W", 0), ("S", 0), ("U", 0), ("A2", 1)]
    for i in range(nz):
        ops.append(("D", i))
        if i + 2 < nz:
            ops.append(("A1", i + 2))
        if i + 1 < nz:
            ops += [("A3", i + 1)]
        if i >= 1:
            ops.append(("L", i - 1))
        if i + 1 < nz:
            ops += [("W", i + 1), ("U", i + 1)]
        if i + 2 < nz:
            ops.append(("A2", i + 2))
        if i >= 2:
            ops.append(("F", i - 2))
        if i >= 3:
            ops.append(("Z", i - 3))
    rest = [("L", nz - 1), ("F", nz - 2), ("Z", nz - 3), ("F", nz - 1), ("Z", nz - 2), ("Z", nz - 1)]
    return ops + [op for op in rest if op[1] >= 0]


def kernel(lay, experts, tok_in, ids_in, rw_in, wg_in, wu_in, wd_in, sg_in, su_in, sd_in, out,
           tok, part, ids, rw, recvp, recvb0, recvb1, recva0, recva1, recvz, hid, hs,
           wg, wu, wd, sg, su, sd, load_sem, tok_send, tok_recv, red_send, pair_recv, b_recv, a_recv, z_recv):
    nz, ny, nt = lay.nz, lay.ny, lay.nt
    rows, width, chips = lay.rows, lay.width, lay.chips
    e_idx, t, p = lax.axis_index("expert"), lax.axis_index("tensor"), lax.axis_index("pair")
    z, y = e_idx // ny, e_idx % ny
    other = 1 - p
    seq = lay.sequence(z)

    def device(z_, y_, t_):
        return {"expert": z_ * ny + y_, "tensor": t_, "pair": p}

    partner = {"expert": e_idx, "tensor": t, "pair": other}
    t_peers = [(t + d) % nt for d in range(1, nt)]
    y_peers = [(y + d) % ny for d in range(1, ny)]

    barrier = pltpu.get_barrier_semaphore()

    def greet(dev):
        pl.semaphore_signal(barrier, inc=1, device_id=dev, device_id_type=MESH)

    for d in range(1, nz):
        greet(device((z + d) % nz, y, t))
    for t_ in t_peers:
        greet(device(z, y, t_))
    for y_ in y_peers:
        greet(device(z, y_, t))
    greet(partner)

    def place(q, z_, y_, t_):
        return ((z_ * 2 + q) * ny + y_) * nt + t_

    cols = [pl.ds(a, n) for a, n in lay.cols]
    wide = [pl.ds(a, n) for a, n in lay.wide]
    slices = range(len(cols))
    first_peers, last_peers = (t_peers, y_peers), (y_peers, t_peers)
    first_at, last_at = (t, y), (y, t)

    def yt(h, first_, last_):
        return (last_, first_) if h == 0 else (first_, last_)

    own = place(p, z, y, t)
    first = pltpu.make_async_copy(tok_in, tok.at[own, :, pl.ds(0, width)], load_sem.at[6])
    small = [pltpu.make_async_copy(ids_in, ids, load_sem.at[7]), pltpu.make_async_copy(rw_in, rw, load_sem.at[8])]
    for load in small:
        load.start()
    first.start()
    loads = [
        pltpu.make_async_copy(src, dst, load_sem.at[i])
        for i, (src, dst) in enumerate(
            ((sg_in, sg), (su_in, su), (wg_in.at[0], wg), (wu_in.at[0], wu), (wd_in.at[0], wd), (sd_in, sd))
        )
    ]
    for load in loads:
        load.start()

    for load in small:
        load.wait()
    lane = lax.broadcasted_iota(jnp.int32, (lay.extra, rows), 0)
    pieces = [jnp.zeros(lane.shape, F32) for _ in range(3)]
    for k in range(ids.shape[0]):
        for m in range(3):
            pieces[m] = pieces[m] + jnp.where(lane == ids[k : k + 1, :] + m * experts, rw[k : k + 1, :], 0.0)
    hi = [v.astype(BF16).astype(F32) for v in pieces]
    rest = [v - h for v, h in zip(pieces, hi)]
    mid = [v.astype(BF16).astype(F32) for v in rest]
    low = [v - h for v, h in zip(rest, mid)]
    mixed = (hi[0] + mid[1] + low[2]).astype(BF16)
    eye = (
        lax.broadcasted_iota(jnp.int32, (rows, rows), 0) == lax.broadcasted_iota(jnp.int32, (rows, rows), 1)
    ).astype(F32).astype(BF16)
    turned = lax.dot_general(eye, mixed, (((1,), (1,)), ((), ())), preferred_element_type=F32)
    tok[own, :, pl.ds(width, lay.extra)] = turned.astype(BF16)

    first.wait()
    pl.semaphore_wait(barrier, nt + ny + nz - 2)

    sent = []

    def send(src, dst, sem_send, sem_recv, dev):
        copy = pltpu.make_async_remote_copy(
            src_ref=src, dst_ref=dst, send_sem=sem_send, recv_sem=sem_recv, device_id=dev, device_id_type=MESH)
        copy.start()
        sent.append(copy)

    def got(dst, sem_recv):
        pltpu.make_async_remote_copy(
            src_ref=dst, dst_ref=dst, send_sem=red_send.at[0], recv_sem=sem_recv,
            device_id=partner, device_id_type=MESH).wait_recv()

    counter = [0]

    def send_block(h, idx, dev):
        view = tok.at[idx, :, wide[h]]
        send(view, view, tok_send.at[counter[0]], tok_recv.at[h, idx], dev)
        counter[0] += 1

    def arrive(h, idx):
        got(tok.at[idx, :, wide[h]], tok_recv.at[h, idx])

    def last_sends(h, idx):
        for v in last_peers[h]:
            send_block(h, idx, device(z, *yt(h, first_at[h], v)))

    def line_step(i):
        blk = place(p, seq[i], y, t)
        for h in slices:
            if i:
                arrive(h, blk)
            for v in first_peers[h]:
                send_block(h, blk, device(z, *yt(h, v, last_at[h])))
        for h in slices:
            last_sends(h, blk)
            send_block(h, blk, partner)

    def first_step(i):
        for h in slices:
            for f in first_peers[h]:
                blk = place(p, seq[i], *yt(h, f, last_at[h]))
                arrive(h, blk)
                last_sends(h, blk)
                send_block(h, blk, partner)

    def last_step(i):
        for h in slices:
            for f in [first_at[h]] + first_peers[h]:
                for v in last_peers[h]:
                    blk = place(p, seq[i], *yt(h, f, v))
                    arrive(h, blk)
                    send_block(h, blk, partner)

    def partner_wait(i):
        for y_ in range(ny):
            for t_ in range(nt):
                for h in slices:
                    arrive(h, place(other, seq[i], y_, t_))

    def hidden_tiles(x, w1, w2, scale, store):
        tile = tile_of(w1.shape[1], 512)
        for n in range(w1.shape[1] // tile):
            at = pl.ds(n * tile, tile)
            g = jnp.dot(x, w1[:, at], preferred_element_type=F32)
            u = jnp.dot(x, w2[:, at], preferred_element_type=F32)
            h = g / (1.0 + jnp.exp(-g)) * u
            if scale is not None:
                h = h * scale
            store[:, at] = h.astype(BF16)

    group = [place(q, z, y, t_) for q in range(2) for t_ in range(nt)]

    def shared_up(_):
        loads[0].wait()
        loads[1].wait()
        x = jnp.concatenate([tok[idx, :, pl.ds(0, width)] for idx in group], axis=0)
        hidden_tiles(x, sg, su, None, hs)

    mine = e_idx * 2 + p

    def up(i):
        if i == 0:
            loads[2].wait()
            loads[3].wait()
        at = pl.ds(seq[i] * lay.plane, lay.plane)
        extra = tok[at, :, pl.ds(width, lay.extra)].reshape(lay.plane * rows, lay.extra)
        l2 = lax.broadcasted_iota(jnp.int32, extra.shape, 1)
        pick = (l2 == mine) | (l2 == mine + experts) | (l2 == mine + 2 * experts)
        scale = jnp.sum(jnp.where(pick, extra.astype(F32), 0.0), axis=1, keepdims=True)
        hidden_tiles(tok[at, :, pl.ds(0, width)].reshape(lay.plane * rows, width), wg, wu, scale, hid)

    def down(i):
        if i == 0:
            loads[4].wait()
            loads[5].wait()
        zi = seq[i]
        for h in slices:
            v = jnp.dot(hid[...], wd[:, cols[h]], preferred_element_type=F32)
            part[pl.ds(zi * lay.plane, lay.plane), :, cols[h]] = v.astype(BF16).reshape(lay.plane, rows, lay.cols[h][1])
            if i == 0:
                v = jnp.dot(hs[...], sd[:, cols[h]], preferred_element_type=F32)
                for j, idx in enumerate(group):
                    part[idx, :, cols[h]] = (part[idx, :, cols[h]].astype(F32) + v[j * rows : (j + 1) * rows]).astype(BF16)
            send_sum(
                part.at[pl.ds(place(other, zi, 0, 0), chips), :, cols[h]],
                recvp.at[pl.ds(zi * chips, chips), :, cols[h]], pair_recv.at[h, zi], partner)

    rcount = [0]

    def send_sum(src, dst, sem_recv, dev):
        send(src, dst, red_send.at[rcount[0]], sem_recv, dev)
        rcount[0] += 1

    recvb, recva = (recvb0, recvb1), (recva0, recva1)

    def buf_b(h, d, z_, f):
        at = (d * nz + z_) * lay.first[h] + f
        return recvb[h].at[at], b_recv.at[h, at]

    def buf_a(h, d, z_):
        at = d * nz + z_
        return recva[h].at[at], a_recv.at[h, at]

    def buf_z(h, d):
        return recvz.at[d, :, cols[h]], z_recv.at[h, d]

    def add_into(h, idx, others):
        v = part[idx, :, cols[h]].astype(F32)
        for ref in others:
            v = v + ref[...].astype(F32)
        part[idx, :, cols[h]] = v.astype(BF16)

    def mine_of(z_, y_, t_, h):
        return recvp.at[(z_ * ny + y_) * nt + t_, :, cols[h]]

    def sums_last(i):
        z_ = seq[i]
        for h in slices:
            got(recvp.at[pl.ds(z_ * chips, chips), :, cols[h]], pair_recv.at[h, z_])
            for f in first_peers[h] + [first_at[h]]:
                for d, v in enumerate(last_peers[h]):
                    y_, t_ = yt(h, f, v)
                    idx = place(p, z_, y_, t_)
                    add_into(h, idx, [mine_of(z_, y_, t_, h)])
                    ref, sem = buf_b(h, d, z_, f)
                    send_sum(part.at[idx, :, cols[h]], ref, sem, device(z, *yt(h, first_at[h], v)))

    def collect_last(h, z_, f):
        y_, t_ = yt(h, f, last_at[h])
        refs = [mine_of(z_, y_, t_, h)]
        for d in range(lay.last[h] - 1):
            ref, sem = buf_b(h, d, z_, f)
            got(ref, sem)
            refs.append(ref)
        return place(p, z_, y_, t_), refs

    def sums_first(i):
        z_ = seq[i]
        for h in slices:
            for d, f in enumerate(first_peers[h]):
                idx, refs = collect_last(h, z_, f)
                add_into(h, idx, refs)
                ref, sem = buf_a(h, d, z_)
                send_sum(part.at[idx, :, cols[h]], ref, sem, device(z, *yt(h, f, last_at[h])))

    def sums_line(i):
        z_ = seq[i]
        for h in slices:
            idx, refs = collect_last(h, z_, first_at[h])
            for d in range(lay.first[h] - 1):
                ref, sem = buf_a(h, d, z_)
                got(ref, sem)
                refs.append(ref)
            add_into(h, idx, refs)
            if i:
                ref, sem = buf_z(h, (z_ - z + nz) % nz - 1)
                send_sum(part.at[idx, :, cols[h]], ref, sem, device(z_, y, t))

    line_order = [i for i in range(1, nz)]
    for i in line_order:
        for h in slices:
            send_block(h, own, device(seq[i], y, t))
    line_step(0)
    steps = {
        "A1": line_step, "A2": first_step, "A3": last_step, "W": partner_wait, "S": shared_up, "U": up, "D": down,
        "L": sums_last, "F": sums_first, "Z": sums_line,
    }
    for name, i in schedule(nz):
        steps[name](i)

    for h in slices:
        v = part[own, :, cols[h]].astype(F32)
        for d in range(nz - 1):
            ref, sem = buf_z(h, d)
            got(ref, sem)
            v = v + ref[...].astype(F32)
        out[:, cols[h]] = v.astype(BF16)
    for copy in sent:
        copy.wait_send()


def per_device(lay, experts, tokens, ids, rw, wg, wu, wd, sg, su, sd):
    rows, width = tokens.shape
    nz, ny, nt = lay.nz, lay.ny, lay.nt
    hidden, shared = wg.shape[2], sg.shape[1]
    n = len(lay.cols)
    sends = n * (nz - 1 + nz * (nt - 1 + ny - 1 + 1) + nz * (nt - 1 + ny - 1 + nt * ny) + nz * 2 * nt * ny) + n * nz * nt * ny
    red = n * nz * (1 + 2 * nt * ny + nt + ny + 1)
    many_b = [max(1, (lay.last[h] - 1) * nz * lay.first[h]) for h in range(2)]
    many_a = [max(1, (lay.first[h] - 1) * nz) for h in range(2)]
    halves = [c[1] for c in lay.cols]
    vmem = pl.BlockSpec(memory_space=pltpu.VMEM)
    anyw = pl.BlockSpec(memory_space=pl.ANY)
    scratch = [
        pltpu.VMEM((lay.blocks, rows, width + lay.extra), BF16),
        pltpu.VMEM((lay.blocks, rows, width), BF16),
        pltpu.VMEM(ids.shape, jnp.int32),
        pltpu.VMEM(rw.shape, F32),
        pltpu.VMEM((lay.blocks // 2, rows, width), BF16),
        pltpu.VMEM((many_b[0], rows, halves[0]), BF16),
        pltpu.VMEM((many_b[1], rows, halves[1]), BF16),
        pltpu.VMEM((many_a[0], rows, halves[0]), BF16),
        pltpu.VMEM((many_a[1], rows, halves[1]), BF16),
        pltpu.VMEM((max(1, nz - 1), rows, width), BF16),
        pltpu.VMEM((lay.plane * rows, hidden), BF16),
        pltpu.VMEM((2 * nt * rows, shared), BF16),
        pltpu.VMEM(wg.shape[1:], BF16),
        pltpu.VMEM(wu.shape[1:], BF16),
        pltpu.VMEM(wd.shape[1:], BF16),
        pltpu.VMEM(sg.shape, BF16),
        pltpu.VMEM(su.shape, BF16),
        pltpu.VMEM(sd.shape, BF16),
        pltpu.SemaphoreType.DMA((9,)),
        pltpu.SemaphoreType.DMA((sends,)),
        pltpu.SemaphoreType.DMA((n, lay.blocks)),
        pltpu.SemaphoreType.DMA((red,)),
        pltpu.SemaphoreType.DMA((n, nz)),
        pltpu.SemaphoreType.DMA((2, max(many_b))),
        pltpu.SemaphoreType.DMA((2, max(many_a))),
        pltpu.SemaphoreType.DMA((n, max(1, nz - 1))),
    ]
    return pl.pallas_call(
        functools.partial(kernel, lay, experts),
        out_shape=jax.ShapeDtypeStruct((rows, width), BF16),
        in_specs=[anyw] * 9,
        out_specs=vmem,
        scratch_shapes=scratch,
        compiler_params=pltpu.CompilerParams(
            collective_id=0, has_side_effects=True, vmem_limit_bytes=67043328
        ),
    )(tokens, ids, rw, wg, wu, wd, sg, su, sd)


def solution(mesh):
    shape = dict(mesh.shape)

    def body(tokens, ids, rw, wg, wu, wd, sg, su, sd):
        experts = shape["expert"] * shape["pair"] * wg.shape[0]
        lay = Layout(shape["expert"], shape["tensor"], tokens.shape[0], tokens.shape[1], experts)
        return per_device(lay, experts, tokens, ids.T, rw.T, wg, wu, wd, sg, su, sd)

    in_specs = (
        P(("groups", "expert", "tensor", "pair"), None),
        P(("groups", "expert", "tensor", "pair"), None),
        P(("groups", "expert", "tensor", "pair"), None),
        P(("expert", "pair"), None, "tensor"),
        P(("expert", "pair"), None, "tensor"),
        P(("expert", "pair"), "tensor", None),
        P(None, ("tensor", "pair")),
        P(None, ("tensor", "pair")),
        P(("tensor", "pair"), None),
    )
    out_specs = P(("groups", "expert", "tensor", "pair"), None)
    return jax.shard_map(body, mesh=mesh, in_specs=in_specs, out_specs=out_specs, check_vma=False)
```

time: 68.6 us -> 61.5 us (0.90)
  Pallas kernels: 64.1 us -> 59.8 us
  local copies, waits for them, and re-layouts: 4.26 us -> 1.55 us
    pallas_call x1, Pallas kernels: 64.1 us -> 59.8 us  [per_device(): pl.pallas_call(functools.partial(kernel, lay, experts), out_shape=jax.Sha...]
    unnamed x3 -> x1, local copies, waits for them, and re-layouts: 4.26 us -> 1.55 us
where the time goes in v1:
time: 61.5 us; the launch traced here: 61.4 us
  Pallas kernels  59.8 us (97%)
  local copies, waits for them, and re-layouts  1.55 us (3%)
    pallas_call x1, Pallas kernels, per_device(): pl.pallas_call(functools.partial(kernel, lay, experts), out_shape=jax.Sha...  59.8 us
    unnamed x1, local copies, waits for them, and re-layouts  1.55 us

profile of v1, /device:TPU:0, one launch (start us, length us, event | category | flops | bytes accessed | tf_op | source)
XLA Modules:
  0.0 61.4 jit_solution(6533462932515390509)
XLA Ops:
  0.0 59.8 %shard_map.91 = bf16[16,3584]{1,0:T(8,128)(2,1)} custom-call(bf16[16,3584]{1,0:T(8,128)(2,1)} %tok_in.1, s32[8,16]{1,0:T(8,128)} %bitcast.2, f32[8,16]{1,0:T(8,128)} %bitcast.3, bf16[1,3584,512]{2,1,0:T(8,128)(2,1)} %wg_in.1, bf16[1,3584,512]{2,1,0:T(8,128)(2,1)} %wu_in.1, bf16[1,512,3584]{2,1,0:T(8,128)(2,1)} %wd_in.1, bf16[3584,512]{1,0:T(8,128)(2,1)} %sg_in.1, ...), custom_call_target="tpu_custom_call" | custom-call | tf_op jit(solution)/shard_map/pallas_call | solution.py:394
  59.8 1.6 %copy.11 = bf16[16,3584]{1,0:T(8,128)(2,1)} copy(bf16[16,3584]{1,0:T(8,128)(2,1)} %shard_map.91) | data formatting | bytes 229376

commit v2 on v1

v2 whole, which is shorter than its diff:
```python
import functools

import jax
import jax.numpy as jnp
from jax import lax
from jax.experimental import pallas as pl
from jax.experimental.pallas import tpu as pltpu
from jax.sharding import PartitionSpec as P

MESH = pl.DeviceIdType.MESH
F32 = jnp.float32
BF16 = jnp.bfloat16


def lanes_for(experts):
    return -(-3 * experts // 128) * 128


def tile_of(width, most):
    for tile in range(min(width, most), 0, -1):
        if width % tile == 0 and (tile % 128 == 0 or tile == width):
            return tile
    return width


class Layout:
    def __init__(self, n_expert, n_tensor, tok_rows, width, experts):
        self.nt = n_tensor
        self.ny = 2 if n_expert % 2 == 0 else 1
        self.nz = n_expert // self.ny
        self.chips = self.ny * self.nt
        self.plane = 2 * self.chips
        self.blocks = self.nz * self.plane
        self.rows, self.width, self.extra = tok_rows, width, lanes_for(experts)
        units, at, self.cols = width // 128, 0, []
        for h in range(SLICES):
            n = (units * (h + 1) // SLICES - units * h // SLICES) * 128
            if h == SLICES - 1:
                n = width - at
            self.cols.append((at, n))
            at += n
        self.wide = self.cols[:-1] + [(self.cols[-1][0], self.cols[-1][1] + self.extra)]
        self.first = [(self.nt, self.ny)[h % 2] for h in range(SLICES)]
        self.last = [(self.ny, self.nt)[h % 2] for h in range(SLICES)]

    def sequence(self, z):
        nz = self.nz
        m = jnp.minimum(z, nz - 1 - z)
        out = [z]
        for i in range(1, nz):
            near = z + (i + 1) // 2 if i % 2 else z - i // 2
            far = jnp.where(z <= nz - 1 - z, z + (i - m), z - (i - m))
            out.append(jnp.where(i <= 2 * m, near, far))
        return out


SLICES = 2


def schedule(nz):
    ops = [("A2", 0), ("A1", 1), ("A1", 2), ("A3", 0), ("A2", 1), ("W", 0), ("S", 0), ("U", 0)]
    done = set()
    for i in range(nz):
        ops += [("A1", i + 3), ("A2", i + 2)]
        if i + 2 < nz:
            ops += [("A3", i + 1), ("D", i), ("W", i + 1), ("U", i + 1)]
        elif i + 1 < nz:
            ops += [("L", i - 1), ("D", i)] + [("L", j) for j in range(i - 1)]
            ops += [("A3", i + 1), ("L", i), ("W", i + 1), ("U", i + 1)]
        else:
            ops += [("D", i)]
    for j in range(1, nz - 1):
        ops.append(("F", j))
    ops.append(("L", nz - 1))
    for j in range(1, nz - 1):
        ops.append(("Z", j))
    ops += [("F", 0), ("F", nz - 1), ("Z", nz - 1), ("Z", 0)]
    out = []
    for op in ops:
        if 0 <= op[1] < nz and op not in out:
            out.append(op)
    return out


def kernel(lay, experts, tok_in, ids_in, rw_in, wg_in, wu_in, wd_in, sg_in, su_in, sd_in, out,
           tok, part, ids, rw, recvp, recvb, recva, recvz, hid, hs, wg, wu, wd, sg, su, sd,
           load_sem, bulk_send, line_send, line_recv, first_recv, last_recv, swap_recv, pair_recv, b_recv, a_recv, z_recv):
    nz, ny, nt = lay.nz, lay.ny, lay.nt
    rows, width, chips = lay.rows, lay.width, lay.chips
    e_idx, t, p = lax.axis_index("expert"), lax.axis_index("tensor"), lax.axis_index("pair")
    z, y = e_idx // ny, e_idx % ny
    other = 1 - p
    seq = lay.sequence(z)

    def device(z_, y_, t_):
        return {"expert": z_ * ny + y_, "tensor": t_, "pair": p}

    partner = {"expert": e_idx, "tensor": t, "pair": other}
    t_peers = [(t + d) % nt for d in range(1, nt)]
    y_peers = [(y + d) % ny for d in range(1, ny)]

    barrier = pltpu.get_barrier_semaphore()

    def greet(dev):
        pl.semaphore_signal(barrier, inc=1, device_id=dev, device_id_type=MESH)

    for d in range(1, nz):
        greet(device((z + d) % nz, y, t))
    for t_ in t_peers:
        greet(device(z, y, t_))
    for y_ in y_peers:
        greet(device(z, y_, t))
    greet(partner)

    def place(q, z_, y_, t_):
        return ((z_ * 2 + q) * ny + y_) * nt + t_

    cols = [pl.ds(a, n) for a, n in lay.cols]
    wide = [pl.ds(a, n) for a, n in lay.wide]
    slices = range(len(cols))
    first_peers = [(t_peers, y_peers)[h % 2] for h in slices]
    last_peers = [(y_peers, t_peers)[h % 2] for h in slices]
    first_at = [(t, y)[h % 2] for h in slices]
    last_at = [(y, t)[h % 2] for h in slices]

    def yt(h, first_, last_):
        return (last_, first_) if h % 2 == 0 else (first_, last_)

    own = place(p, z, y, t)
    first = pltpu.make_async_copy(tok_in, tok.at[own, :, pl.ds(0, width)], load_sem.at[6])
    small = [pltpu.make_async_copy(ids_in, ids, load_sem.at[7]), pltpu.make_async_copy(rw_in, rw, load_sem.at[8])]
    for load in small:
        load.start()
    first.start()
    loads = [
        pltpu.make_async_copy(src, dst, load_sem.at[i])
        for i, (src, dst) in enumerate(
            ((sg_in, sg), (su_in, su), (wg_in.at[0], wg), (wu_in.at[0], wu), (wd_in.at[0], wd), (sd_in, sd))
        )
    ]
    for load in loads:
        load.start()

    for load in small:
        load.wait()
    lane = lax.broadcasted_iota(jnp.int32, (lay.extra, rows), 0)
    pieces = [jnp.zeros(lane.shape, F32) for _ in range(3)]
    for k in range(ids.shape[0]):
        for m in range(3):
            pieces[m] = pieces[m] + jnp.where(lane == ids[k : k + 1, :] + m * experts, rw[k : k + 1, :], 0.0)
    hi = [v.astype(BF16).astype(F32) for v in pieces]
    rest = [v - h for v, h in zip(pieces, hi)]
    mid = [v.astype(BF16).astype(F32) for v in rest]
    low = [v - h for v, h in zip(rest, mid)]
    mixed = (hi[0] + mid[1] + low[2]).astype(BF16)
    eye = (
        lax.broadcasted_iota(jnp.int32, (rows, rows), 0) == lax.broadcasted_iota(jnp.int32, (rows, rows), 1)
    ).astype(F32).astype(BF16)
    turned = lax.dot_general(eye, mixed, (((1,), (1,)), ((), ())), preferred_element_type=F32)
    tok[own, :, pl.ds(width, lay.extra)] = turned.astype(BF16)

    first.wait()
    pl.semaphore_wait(barrier, nt + ny + nz - 2)

    def remote(src, dst, sem_send, sem_recv, dev):
        return pltpu.make_async_remote_copy(
            src_ref=src, dst_ref=dst, send_sem=sem_send, recv_sem=sem_recv, device_id=dev, device_id_type=MESH)

    def got(view, sem_recv):
        remote(view, view, bulk_send.at[0, 0], sem_recv, partner).wait_recv()

    counts = {}

    def send(kind, h, src, dst, sem_recv, dev, blocks=1):
        remote(src, dst, bulk_send.at[kind, h], sem_recv, dev).start()
        counts[kind, h] = counts.get((kind, h), 0) + blocks

    def send_block(kind, h, idx, sem_recv, dev):
        view = tok.at[idx, :, wide[h]]
        send(kind, h, view, view, sem_recv, dev)

    line_sent = []

    def send_line(slot, idx, z_, target):
        ok = (target >= 0) & (target < nz)
        dev = device(target, y, t)

        def whole():
            remote(tok.at[idx], tok.at[idx], line_send.at[slot], line_recv.at[0, 0], dev).wait_send()

        def part_of(h):
            view = tok.at[idx, :, wide[h]]
            pl.when(ok)(remote(view, view, line_send.at[slot], line_recv.at[h, z_], dev).start)

        line_sent.append((ok, whole))
        return part_of

    def last_sends(h, idx, z_):
        for v in last_peers[h]:
            send_block(1, h, idx, last_recv.at[h, z_], device(z, *yt(h, first_at[h], v)))

    def swap(h, idx, z_):
        send_block(2, h, idx, swap_recv.at[z_], partner)

    def line_step(i):
        z_ = seq[i]
        blk = place(p, z_, y, t)
        if i == 0:
            onward = [send_line(0, blk, z_, z + 1), send_line(nz, blk, z_, z - 1)]
        else:
            onward = [send_line(i, blk, z_, jnp.where(z_ < z, z + 1, z - 1))]
        for h in slices:
            if i:
                got(tok.at[blk, :, wide[h]], line_recv.at[h, z_])
            for part_of in onward:
                part_of(h)
            for d, v in enumerate(first_peers[h]):
                send_block(0, h, blk, first_recv.at[h, d * nz + z_], device(z, *yt(h, v, last_at[h])))
        for h in slices:
            last_sends(h, blk, z_)
            swap(h, blk, z_)

    def first_step(i):
        z_ = seq[i]
        for h in slices:
            n = lay.first[h]
            for d in range(n - 1):
                f = (first_at[h] + n - 1 - d) % n
                blk = place(p, z_, *yt(h, f, last_at[h]))
                got(tok.at[blk, :, wide[h]], first_recv.at[h, d * nz + z_])
                last_sends(h, blk, z_)
                swap(h, blk, z_)

    def last_step(i):
        z_ = seq[i]
        for h in slices:
            n = lay.first[h] * (lay.last[h] - 1)
            if n:
                got(tok.at[pl.ds(0, n), :, wide[h]], last_recv.at[h, z_])
            for f in [first_at[h]] + first_peers[h]:
                for v in last_peers[h]:
                    swap(h, place(p, z_, *yt(h, f, v)), z_)

    def partner_wait(i):
        got(tok.at[pl.ds(place(other, seq[i], 0, 0), chips)], swap_recv.at[seq[i]])

    def hidden_tiles(x, w1, w2, scale, store):
        tile = tile_of(w1.shape[1], 512)
        for n in range(w1.shape[1] // tile):
            at = pl.ds(n * tile, tile)
            g = jnp.dot(x, w1[:, at], preferred_element_type=F32)
            u = jnp.dot(x, w2[:, at], preferred_element_type=F32)
            h = g / (1.0 + jnp.exp(-g)) * u
            if scale is not None:
                h = h * scale
            store[:, at] = h.astype(BF16)

    group = [place(q, z, y, t_) for q in range(2) for t_ in range(nt)]

    def shared_up(_):
        loads[0].wait()
        loads[1].wait()
        x = jnp.concatenate([tok[idx, :, pl.ds(0, width)] for idx in group], axis=0)
        hidden_tiles(x, sg, su, None, hs)

    mine = e_idx * 2 + p

    def up(i):
        if i == 0:
            loads[2].wait()
            loads[3].wait()
        at = pl.ds(seq[i] * lay.plane, lay.plane)
        extra = tok[at, :, pl.ds(width, lay.extra)].reshape(lay.plane * rows, lay.extra)
        l2 = lax.broadcasted_iota(jnp.int32, extra.shape, 1)
        pick = (l2 == mine) | (l2 == mine + experts) | (l2 == mine + 2 * experts)
        scale = jnp.sum(jnp.where(pick, extra.astype(F32), 0.0), axis=1, keepdims=True)
        hidden_tiles(tok[at, :, pl.ds(0, width)].reshape(lay.plane * rows, width), wg, wu, scale, hid)

    def down(i):
        if i == 0:
            loads[4].wait()
            loads[5].wait()
        z_ = seq[i]
        for h in slices:
            v = jnp.dot(hid[...], wd[:, cols[h]], preferred_element_type=F32)
            part[pl.ds(z_ * lay.plane, lay.plane), :, cols[h]] = v.astype(BF16).reshape(lay.plane, rows, lay.cols[h][1])
            if i == 0:
                v = jnp.dot(hs[...], sd[:, cols[h]], preferred_element_type=F32)
                for j, idx in enumerate(group):
                    part[idx, :, cols[h]] = (part[idx, :, cols[h]].astype(F32) + v[j * rows : (j + 1) * rows]).astype(BF16)
            send(3, h, part.at[pl.ds(place(other, z_, 0, 0), chips), :, cols[h]],
                 recvp.at[pl.ds(z_ * chips, chips), :, cols[h]], pair_recv.at[h, z_], partner, chips)

    def buf_b(h, d, z_, f):
        return recvb.at[(d * nz + z_) * lay.first[h] + f, :, cols[h]]

    def buf_a(h, d, z_):
        return recva.at[d * nz + z_, :, cols[h]]

    def add_into(h, idx, others):
        v = part[idx, :, cols[h]].astype(F32)
        for ref in others:
            v = v + ref[...].astype(F32)
        part[idx, :, cols[h]] = v.astype(BF16)

    def mine_of(z_, y_, t_, h):
        return recvp.at[(z_ * ny + y_) * nt + t_, :, cols[h]]

    def sums_last(i):
        z_ = seq[i]
        for h in slices:
            got(recvp.at[pl.ds(z_ * chips, chips), :, cols[h]], pair_recv.at[h, z_])
            for k, f in enumerate(first_peers[h] + [first_at[h]]):
                here = int(k == lay.first[h] - 1)
                for d, v in enumerate(last_peers[h]):
                    y_, t_ = yt(h, f, v)
                    idx = place(p, z_, y_, t_)
                    add_into(h, idx, [mine_of(z_, y_, t_, h)])
                    send(4, h, part.at[idx, :, cols[h]], buf_b(h, d, z_, f), b_recv.at[h, here * nz + z_],
                         device(z, *yt(h, first_at[h], v)))

    def collect_last(h, z_, f):
        y_, t_ = yt(h, f, last_at[h])
        return place(p, z_, y_, t_), [mine_of(z_, y_, t_, h)] + [buf_b(h, d, z_, f) for d in range(lay.last[h] - 1)]

    def sums_first(i):
        z_ = seq[i]
        for h in slices:
            n = (lay.first[h] - 1) * (lay.last[h] - 1)
            if n:
                got(recvb.at[pl.ds(0, n), :, cols[h]], b_recv.at[h, z_])
            for d, f in enumerate(first_peers[h]):
                idx, refs = collect_last(h, z_, f)
                add_into(h, idx, refs)
                send(5, h, part.at[idx, :, cols[h]], buf_a(h, d, z_), a_recv.at[h, z_], device(z, *yt(h, f, last_at[h])))

    def sums_line(i):
        z_ = seq[i]
        for h in slices:
            if lay.last[h] > 1:
                got(recvb.at[pl.ds(0, lay.last[h] - 1), :, cols[h]], b_recv.at[h, nz + z_])
            if lay.first[h] > 1:
                got(recva.at[pl.ds(0, lay.first[h] - 1), :, cols[h]], a_recv.at[h, z_])
            idx, refs = collect_last(h, z_, first_at[h])
            add_into(h, idx, refs + [buf_a(h, d, z_) for d in range(lay.first[h] - 1)])
            if i:
                slot = (z_ - z + nz) % nz - 1
                send(6, h, part.at[idx, :, cols[h]], recvz.at[slot, :, cols[h]], z_recv.at[h], device(z_, y, t))

    line_step(0)
    steps = {
        "A1": line_step, "A2": first_step, "A3": last_step, "W": partner_wait, "S": shared_up, "U": up, "D": down,
        "L": sums_last, "F": sums_first, "Z": sums_line,
    }
    for name, i in schedule(nz):
        steps[name](i)

    for h in slices:
        if nz > 1:
            got(recvz.at[pl.ds(0, nz - 1), :, cols[h]], z_recv.at[h])
        v = part[own, :, cols[h]].astype(F32)
        for d in range(nz - 1):
            v = v + recvz[d, :, cols[h]].astype(F32)
        out[:, cols[h]] = v.astype(BF16)
    for ok, whole in line_sent:
        pl.when(ok)(whole)
    for (kind, h), n in counts.items():
        view = (tok if kind < 3 else part).at[pl.ds(0, n), :, (wide if kind < 3 else cols)[h]]
        remote(view, view, bulk_send.at[kind, h], z_recv.at[h], partner).wait_send()


def per_device(lay, experts, tokens, ids, rw, wg, wu, wd, sg, su, sd):
    rows, width = tokens.shape
    nz, ny, nt = lay.nz, lay.ny, lay.nt
    hidden, shared = wg.shape[2], sg.shape[1]
    n, most = len(lay.cols), max(nt, ny)
    many_b = max(1, max((lay.last[h] - 1) * lay.first[h] for h in range(n)) * nz)
    many_a = max(1, (most - 1) * nz)
    vmem = pl.BlockSpec(memory_space=pltpu.VMEM)
    anyw = pl.BlockSpec(memory_space=pl.ANY)
    dma = pltpu.SemaphoreType.DMA
    scratch = [
        pltpu.VMEM((lay.blocks, rows, width + lay.extra), BF16),
        pltpu.VMEM((lay.blocks, rows, width), BF16),
        pltpu.VMEM(ids.shape, jnp.int32),
        pltpu.VMEM(rw.shape, F32),
        pltpu.VMEM((lay.blocks // 2, rows, width), BF16),
        pltpu.VMEM((many_b, rows, width), BF16),
        pltpu.VMEM((many_a, rows, width), BF16),
        pltpu.VMEM((max(1, nz - 1), rows, width), BF16),
        pltpu.VMEM((lay.plane * rows, hidden), BF16),
        pltpu.VMEM((2 * nt * rows, shared), BF16),
        pltpu.VMEM(wg.shape[1:], BF16),
        pltpu.VMEM(wu.shape[1:], BF16),
        pltpu.VMEM(wd.shape[1:], BF16),
        pltpu.VMEM(sg.shape, BF16),
        pltpu.VMEM(su.shape, BF16),
        pltpu.VMEM(sd.shape, BF16),
        dma((9,)),
        dma((7, n)),
        dma((nz + 1,)),
        dma((n, nz)),
        dma((n, nz * max(1, most - 1))),
        dma((n, nz)),
        dma((nz,)),
        dma((n, nz)),
        dma((n, 2 * nz)),
        dma((n, nz)),
        dma((n,)),
    ]
    return pl.pallas_call(
        functools.partial(kernel, lay, experts),
        out_shape=jax.ShapeDtypeStruct((rows, width), BF16),
        in_specs=[anyw] * 9,
        out_specs=vmem,
        scratch_shapes=scratch,
        compiler_params=pltpu.CompilerParams(
            collective_id=0, has_side_effects=True, vmem_limit_bytes=67043328
        ),
    )(tokens, ids, rw, wg, wu, wd, sg, su, sd)


def solution(mesh):
    shape = dict(mesh.shape)

    def body(tokens, ids, rw, wg, wu, wd, sg, su, sd):
        experts = shape["expert"] * shape["pair"] * wg.shape[0]
        lay = Layout(shape["expert"], shape["tensor"], tokens.shape[0], tokens.shape[1], experts)
        return per_device(lay, experts, tokens, ids.T, rw.T, wg, wu, wd, sg, su, sd)

    in_specs = (
        P(("groups", "expert", "tensor", "pair"), None),
        P(("groups", "expert", "tensor", "pair"), None),
        P(("groups", "expert", "tensor", "pair"), None),
        P(("expert", "pair"), None, "tensor"),
        P(("expert", "pair"), None, "tensor"),
        P(("expert", "pair"), "tensor", None),
        P(None, ("tensor", "pair")),
        P(None, ("tensor", "pair")),
        P(("tensor", "pair"), None),
    )
    out_specs = P(("groups", "expert", "tensor", "pair"), None)
    return jax.shard_map(body, mesh=mesh, in_specs=in_specs, out_specs=out_specs, check_vma=False)
```

time: 61.5 us -> 54.3 us (0.88)
  Pallas kernels: 59.8 us -> 52.6 us
    pallas_call x1, Pallas kernels: 59.8 us -> 52.6 us  [per_device(): pl.pallas_call(functools.partial(kernel, lay, experts), out_shape=jax.Sha...]
where the time goes in v2:
time: 54.3 us; the launch traced here: 54.1 us
  Pallas kernels  52.6 us (97%)
  local copies, waits for them, and re-layouts  1.55 us (3%)
    pallas_call x1, Pallas kernels, per_device(): pl.pallas_call(functools.partial(kernel, lay, experts), out_shape=jax.Sha...  52.6 us
    unnamed x1, local copies, waits for them, and re-layouts  1.55 us

profile of v2, /device:TPU:0, one launch (start us, length us, event | category | flops | bytes accessed | tf_op | source)
XLA Modules:
  0.0 54.1 jit_solution(399785636725565102)
XLA Ops:
  0.0 52.6 %shard_map.91 = bf16[16,3584]{1,0:T(8,128)(2,1)} custom-call(bf16[16,3584]{1,0:T(8,128)(2,1)} %tok_in.1, s32[8,16]{1,0:T(8,128)} %bitcast.2, f32[8,16]{1,0:T(8,128)} %bitcast.3, bf16[1,3584,512]{2,1,0:T(8,128)(2,1)} %wg_in.1, bf16[1,3584,512]{2,1,0:T(8,128)(2,1)} %wu_in.1, bf16[1,512,3584]{2,1,0:T(8,128)(2,1)} %wd_in.1, bf16[3584,512]{1,0:T(8,128)(2,1)} %sg_in.1, ...), custom_call_target="tpu_custom_call" | custom-call | tf_op jit(solution)/shard_map/pallas_call | solution.py:411
  52.6 1.6 %copy.11 = bf16[16,3584]{1,0:T(8,128)(2,1)} copy(bf16[16,3584]{1,0:T(8,128)(2,1)} %shard_map.91) | data formatting | bytes 229376

commit v3 on v2

--- a/solution.py
+++ b/solution.py
@@ -43,43 +43,42 @@
         self.first = [(self.nt, self.ny)[h % 2] for h in range(SLICES)]
         self.last = [(self.ny, self.nt)[h % 2] for h in range(SLICES)]
 
-    def sequence(self, z):
+    def sequences(self, z):
         nz = self.nz
         m = jnp.minimum(z, nz - 1 - z)
-        out = [z]
+        side = jnp.where(z <= nz - 1 - z, 1, -1)
+        hops, taken = [z], [z]
         for i in range(1, nz):
-            near = z + (i + 1) // 2 if i % 2 else z - i // 2
-            far = jnp.where(z <= nz - 1 - z, z + (i - m), z - (i - m))
-            out.append(jnp.where(i <= 2 * m, near, far))
-        return out
+            near = z + side * ((i + 1) // 2) if i % 2 else z - side * (i // 2)
+            hops.append(jnp.where(i <= 2 * m, near, z + side * (i - m)))
+            moved = z + side * (i + 1 - m) if i < nz - 1 else z - side * m
+            taken.append(jnp.where(m == 0, z + side * i, jnp.where(i < 2 * m, near, moved)))
+        return hops, taken
 
 
 SLICES = 2
 
 
 def schedule(nz):
-    ops = [("A2", 0), ("A1", 1), ("A1", 2), ("A3", 0), ("A2", 1), ("W", 0), ("S", 0), ("U", 0)]
-    done = set()
+    ops = ["A2 0", "R 1", "A1m 1", "A1e 1", "R 2", "A1e 2", "R 3", "A1m 2", "A3 0", "A2 1"]
+    ops += [f"R {i}" for i in range(4, nz)]
+    ops += ["A1m 3", "W 0", "S 0", "U 0"]
     for i in range(nz):
-        ops += [("A1", i + 3), ("A2", i + 2)]
-        if i + 2 < nz:
-            ops += [("A3", i + 1), ("D", i), ("W", i + 1), ("U", i + 1)]
-        elif i + 1 < nz:
-            ops += [("L", i - 1), ("D", i)] + [("L", j) for j in range(i - 1)]
-            ops += [("A3", i + 1), ("L", i), ("W", i + 1), ("U", i + 1)]
-        else:
-            ops += [("D", i)]
-    for j in range(1, nz - 1):
-        ops.append(("F", j))
-    ops.append(("L", nz - 1))
-    for j in range(1, nz - 1):
-        ops.append(("Z", j))
-    ops += [("F", 0), ("F", nz - 1), ("Z", nz - 1), ("Z", 0)]
+        ops += [f"A1m {i + 4}", f"A1e {i + 3}", f"A2 {i + 2}", f"A3 {i + 1}", f"L {i - 1}" if i > 1 else "", f"D {i}"]
+        ops += [f"W {i + 1}", f"A2 {i + 3}", f"U {i + 1}", "L 0"]
+    ops += ["F 1", f"L {nz - 1}"]
+    for j in range(2, nz - 1):
+        ops += [f"F {j}", f"Z {j - 1}"]
+    ops += [f"F {nz - 1}", "F 0", f"Z {nz - 2}", f"Z {nz - 1}", "Z 0"]
+    return tidy(ops, nz)
+
+
+def tidy(ops, nz):
     out = []
     for op in ops:
-        if 0 <= op[1] < nz and op not in out:
+        if op and op not in out and int(op.split()[1]) < nz:
             out.append(op)
-    return out
+    return [(op.split()[0], int(op.split()[1])) for op in out]
 
 
 def kernel(lay, experts, tok_in, ids_in, rw_in, wg_in, wu_in, wd_in, sg_in, su_in, sd_in, out,
@@ -90,7 +89,7 @@
     e_idx, t, p = lax.axis_index("expert"), lax.axis_index("tensor"), lax.axis_index("pair")
     z, y = e_idx // ny, e_idx % ny
     other = 1 - p
-    seq = lay.sequence(z)
+    hops, seq = lay.sequences(z)
 
     def device(z_, y_, t_):
         return {"expert": z_ * ny + y_, "tensor": t_, "pair": p}
@@ -190,7 +189,11 @@
 
         def part_of(h):
             view = tok.at[idx, :, wide[h]]
-            pl.when(ok)(remote(view, view, line_send.at[slot], line_recv.at[h, z_], dev).start)
+            copy = remote(view, view, line_send.at[slot], line_recv.at[h, z_], dev)
+            if slot in (0, nz):
+                pl.when(ok)(copy.start)
+            else:
+                copy.start()
 
         line_sent.append((ok, whole))
         return part_of
@@ -202,23 +205,58 @@
     def swap(h, idx, z_):
         send_block(2, h, idx, swap_recv.at[z_], partner)
 
-    def line_step(i):
-        z_ = seq[i]
+    def inner(z_):
+        target = jnp.where(z_ < z, z + 1, z - 1)
+        return target, (target >= 0) & (target < nz)
+
+    def take(i):
+        blk = place(p, seq[i], y, t)
+        for h in slices:
+            got(tok.at[blk, :, wide[h]], line_recv.at[h, seq[i]])
+
+    def relay_step(i):
+        z_ = hops[i]
+        target, ok = inner(z_)
         blk = place(p, z_, y, t)
-        if i == 0:
-            onward = [send_line(0, blk, z_, z + 1), send_line(nz, blk, z_, z - 1)]
-        else:
-            onward = [send_line(i, blk, z_, jnp.where(z_ < z, z + 1, z - 1))]
-        for h in slices:
-            if i:
+        part_of = send_line(i, blk, z_, target)
+
+        def go():
+            for h in slices:
                 got(tok.at[blk, :, wide[h]], line_recv.at[h, z_])
-            for part_of in onward:
                 part_of(h)
+
+        pl.when(ok)(go)
+
+    def spread(i):
+        z_ = seq[i]
+        blk = place(p, z_, y, t)
+        for h in slices:
             for d, v in enumerate(first_peers[h]):
                 send_block(0, h, blk, first_recv.at[h, d * nz + z_], device(z, *yt(h, v, last_at[h])))
         for h in slices:
             last_sends(h, blk, z_)
             swap(h, blk, z_)
+
+    def inner_step(i):
+        pl.when(inner(seq[i])[1])(lambda: spread(i))
+
+    def outer_step(i):
+        kept = dict(counts)
+
+        def go():
+            take(i)
+            spread(i)
+
+        pl.when(jnp.logical_not(inner(seq[i])[1]))(go)
+        counts.clear()
+        counts.update(kept)
+
+    def start_step():
+        up, down_ = send_line(0, own, z, z + 1), send_line(nz, own, z, z - 1)
+        for h in slices:
+            up(h)
+            down_(h)
+        spread(0)
 
     def first_step(i):
         z_ = seq[i]
@@ -347,9 +385,9 @@
                 slot = (z_ - z + nz) % nz - 1
                 send(6, h, part.at[idx, :, cols[h]], recvz.at[slot, :, cols[h]], z_recv.at[h], device(z_, y, t))
 
-    line_step(0)
+    start_step()
     steps = {
-        "A1": line_step, "A2": first_step, "A3": last_step, "W": partner_wait, "S": shared_up, "U": up, "D": down,
+        "R": relay_step, "A1m": inner_step, "A1e": outer_step, "A2": first_step, "A3": last_step, "W": partner_wait, "S": shared_up, "U": up, "D": down,
         "L": sums_last, "F": sums_first, "Z": sums_line,
     }
     for name, i in schedule(nz):

time: 54.3 us -> 48.5 us (0.89)
  Pallas kernels: 52.6 us -> 46.7 us
    pallas_call x1, Pallas kernels: 52.6 us -> 46.7 us  [per_device(): pl.pallas_call(functools.partial(kernel, lay, experts), out_shape=jax.Sha...]
where the time goes in v3:
time: 48.5 us; the launch traced here: 48.3 us
  Pallas kernels  46.7 us (96%)
  local copies, waits for them, and re-layouts  1.55 us (3%)
    pallas_call x1, Pallas kernels, per_device(): pl.pallas_call(functools.partial(kernel, lay, experts), out_shape=jax.Sha...  46.7 us
    unnamed x1, local copies, waits for them, and re-layouts  1.55 us

profile of v3, /device:TPU:0, one launch (start us, length us, event | category | flops | bytes accessed | tf_op | source)
XLA Modules:
  0.0 48.3 jit_solution(16845087027898381006)
XLA Ops:
  0.0 46.7 %shard_map.91 = bf16[16,3584]{1,0:T(8,128)(2,1)} custom-call(bf16[16,3584]{1,0:T(8,128)(2,1)} %tok_in.1, s32[8,16]{1,0:T(8,128)} %bitcast.2, f32[8,16]{1,0:T(8,128)} %bitcast.3, bf16[1,3584,512]{2,1,0:T(8,128)(2,1)} %wg_in.1, bf16[1,3584,512]{2,1,0:T(8,128)(2,1)} %wu_in.1, bf16[1,512,3584]{2,1,0:T(8,128)(2,1)} %wd_in.1, bf16[3584,512]{1,0:T(8,128)(2,1)} %sg_in.1, ...), custom_call_target="tpu_custom_call" | custom-call | tf_op jit(solution)/shard_map/pallas_call | solution.py:449
  46.8 1.6 %copy.11 = bf16[16,3584]{1,0:T(8,128)(2,1)} copy(bf16[16,3584]{1,0:T(8,128)(2,1)} %shard_map.91) | data formatting | bytes 229376

commit v4 on v3

--- a/solution.py
+++ b/solution.py
@@ -32,16 +32,16 @@
         self.plane = 2 * self.chips
         self.blocks = self.nz * self.plane
         self.rows, self.width, self.extra = tok_rows, width, lanes_for(experts)
-        units, at, self.cols = width // 128, 0, []
-        for h in range(SLICES):
-            n = (units * (h + 1) // SLICES - units * h // SLICES) * 128
-            if h == SLICES - 1:
-                n = width - at
-            self.cols.append((at, n))
-            at += n
-        self.wide = self.cols[:-1] + [(self.cols[-1][0], self.cols[-1][1] + self.extra)]
-        self.first = [(self.nt, self.ny)[h % 2] for h in range(SLICES)]
-        self.last = [(self.ny, self.nt)[h % 2] for h in range(SLICES)]
+        self.wide, self.cols, self.halves = self.cut(GATHER), self.cut(REDUCE), self.cut(2)
+        self.wide[-1] = (self.wide[-1][0], self.wide[-1][1] + self.extra)
+        most = max(GATHER, REDUCE)
+        self.first = [(self.nt, self.ny)[h % 2] for h in range(most)]
+        self.last = [(self.ny, self.nt)[h % 2] for h in range(most)]
+
+    def cut(self, many):
+        units = self.width // 128
+        ends = [units * h // many * 128 for h in range(many)] + [self.width]
+        return [(a, b - a) for a, b in zip(ends[:-1], ends[1:])]
 
     def sequences(self, z):
         nz = self.nz
@@ -56,7 +56,8 @@
         return hops, taken
 
 
-SLICES = 2
+GATHER = 4
+REDUCE = 4
 
 
 def schedule(nz):
@@ -116,7 +117,9 @@
 
     cols = [pl.ds(a, n) for a, n in lay.cols]
     wide = [pl.ds(a, n) for a, n in lay.wide]
-    slices = range(len(cols))
+    halves = [pl.ds(a, n) for a, n in lay.halves]
+    gather, reduce = range(len(wide)), range(len(cols))
+    slices = range(max(len(wide), len(cols)))
     first_peers = [(t_peers, y_peers)[h % 2] for h in slices]
     last_peers = [(y_peers, t_peers)[h % 2] for h in slices]
     first_at = [(t, y)[h % 2] for h in slices]
@@ -200,10 +203,10 @@
 
     def last_sends(h, idx, z_):
         for v in last_peers[h]:
-            send_block(1, h, idx, last_recv.at[h, z_], device(z, *yt(h, first_at[h], v)))
+            send_block(0, h, idx, last_recv.at[h, z_], device(z, *yt(h, first_at[h], v)))
 
     def swap(h, idx, z_):
-        send_block(2, h, idx, swap_recv.at[z_], partner)
+        send_block(1, h, idx, swap_recv.at[z_], partner)
 
     def inner(z_):
         target = jnp.where(z_ < z, z + 1, z - 1)
@@ -211,7 +214,7 @@
 
     def take(i):
         blk = place(p, seq[i], y, t)
-        for h in slices:
+        for h in gather:
             got(tok.at[blk, :, wide[h]], line_recv.at[h, seq[i]])
 
     def relay_step(i):
@@ -221,7 +224,7 @@
         part_of = send_line(i, blk, z_, target)
 
         def go():
-            for h in slices:
+            for h in gather:
                 got(tok.at[blk, :, wide[h]], line_recv.at[h, z_])
                 part_of(h)
 
@@ -230,10 +233,10 @@
     def spread(i):
         z_ = seq[i]
         blk = place(p, z_, y, t)
-        for h in slices:
+        for h in gather:
             for d, v in enumerate(first_peers[h]):
                 send_block(0, h, blk, first_recv.at[h, d * nz + z_], device(z, *yt(h, v, last_at[h])))
-        for h in slices:
+        for h in gather:
             last_sends(h, blk, z_)
             swap(h, blk, z_)
 
@@ -253,14 +256,14 @@
 
     def start_step():
         up, down_ = send_line(0, own, z, z + 1), send_line(nz, own, z, z - 1)
-        for h in slices:
+        for h in gather:
             up(h)
             down_(h)
         spread(0)
 
     def first_step(i):
         z_ = seq[i]
-        for h in slices:
+        for h in gather:
             n = lay.first[h]
             for d in range(n - 1):
                 f = (first_at[h] + n - 1 - d) % n
@@ -271,7 +274,7 @@
 
     def last_step(i):
         z_ = seq[i]
-        for h in slices:
+        for h in gather:
             n = lay.first[h] * (lay.last[h] - 1)
             if n:
                 got(tok.at[pl.ds(0, n), :, wide[h]], last_recv.at[h, z_])
@@ -319,15 +322,15 @@
             loads[4].wait()
             loads[5].wait()
         z_ = seq[i]
-        for h in slices:
-            v = jnp.dot(hid[...], wd[:, cols[h]], preferred_element_type=F32)
-            part[pl.ds(z_ * lay.plane, lay.plane), :, cols[h]] = v.astype(BF16).reshape(lay.plane, rows, lay.cols[h][1])
+        for g, at in enumerate(halves):
+            v = jnp.dot(hid[...], wd[:, at], preferred_element_type=F32)
+            part[pl.ds(z_ * lay.plane, lay.plane), :, at] = v.astype(BF16).reshape(lay.plane, rows, lay.halves[g][1])
             if i == 0:
-                v = jnp.dot(hs[...], sd[:, cols[h]], preferred_element_type=F32)
+                v = jnp.dot(hs[...], sd[:, at], preferred_element_type=F32)
                 for j, idx in enumerate(group):
-                    part[idx, :, cols[h]] = (part[idx, :, cols[h]].astype(F32) + v[j * rows : (j + 1) * rows]).astype(BF16)
-            send(3, h, part.at[pl.ds(place(other, z_, 0, 0), chips), :, cols[h]],
-                 recvp.at[pl.ds(z_ * chips, chips), :, cols[h]], pair_recv.at[h, z_], partner, chips)
+                    part[idx, :, at] = (part[idx, :, at].astype(F32) + v[j * rows : (j + 1) * rows]).astype(BF16)
+            send(2, g, part.at[pl.ds(place(other, z_, 0, 0), chips), :, at],
+                 recvp.at[pl.ds(z_ * chips, chips), :, at], pair_recv.at[g, z_], partner, chips)
 
     def buf_b(h, d, z_, f):
         return recvb.at[(d * nz + z_) * lay.first[h] + f, :, cols[h]]
@@ -344,17 +347,21 @@
     def mine_of(z_, y_, t_, h):
         return recvp.at[(z_ * ny + y_) * nt + t_, :, cols[h]]
 
+    starts = [0, len(cols) // 2]
+
     def sums_last(i):
         z_ = seq[i]
-        for h in slices:
-            got(recvp.at[pl.ds(z_ * chips, chips), :, cols[h]], pair_recv.at[h, z_])
+        for h in reduce:
+            if h in starts:
+                g = starts.index(h)
+                got(recvp.at[pl.ds(z_ * chips, chips), :, halves[g]], pair_recv.at[g, z_])
             for k, f in enumerate(first_peers[h] + [first_at[h]]):
                 here = int(k == lay.first[h] - 1)
                 for d, v in enumerate(last_peers[h]):
                     y_, t_ = yt(h, f, v)
                     idx = place(p, z_, y_, t_)
                     add_into(h, idx, [mine_of(z_, y_, t_, h)])
-                    send(4, h, part.at[idx, :, cols[h]], buf_b(h, d, z_, f), b_recv.at[h, here * nz + z_],
+                    send(3, h, part.at[idx, :, cols[h]], buf_b(h, d, z_, f), (a_recv if here else b_recv).at[h, z_],
                          device(z, *yt(h, first_at[h], v)))
 
     def collect_last(h, z_, f):
@@ -363,27 +370,26 @@
 
     def sums_first(i):
         z_ = seq[i]
-        for h in slices:
+        for h in reduce:
             n = (lay.first[h] - 1) * (lay.last[h] - 1)
             if n:
                 got(recvb.at[pl.ds(0, n), :, cols[h]], b_recv.at[h, z_])
             for d, f in enumerate(first_peers[h]):
                 idx, refs = collect_last(h, z_, f)
                 add_into(h, idx, refs)
-                send(5, h, part.at[idx, :, cols[h]], buf_a(h, d, z_), a_recv.at[h, z_], device(z, *yt(h, f, last_at[h])))
+                send(3, h, part.at[idx, :, cols[h]], buf_a(h, d, z_), a_recv.at[h, z_], device(z, *yt(h, f, last_at[h])))
 
     def sums_line(i):
         z_ = seq[i]
-        for h in slices:
-            if lay.last[h] > 1:
-                got(recvb.at[pl.ds(0, lay.last[h] - 1), :, cols[h]], b_recv.at[h, nz + z_])
-            if lay.first[h] > 1:
-                got(recva.at[pl.ds(0, lay.first[h] - 1), :, cols[h]], a_recv.at[h, z_])
+        for h in reduce:
+            n = lay.last[h] + lay.first[h] - 2
+            if n:
+                got(part.at[pl.ds(0, n), :, cols[h]], a_recv.at[h, z_])
             idx, refs = collect_last(h, z_, first_at[h])
             add_into(h, idx, refs + [buf_a(h, d, z_) for d in range(lay.first[h] - 1)])
             if i:
                 slot = (z_ - z + nz) % nz - 1
-                send(6, h, part.at[idx, :, cols[h]], recvz.at[slot, :, cols[h]], z_recv.at[h], device(z_, y, t))
+                send(3, h, part.at[idx, :, cols[h]], recvz.at[slot, :, cols[h]], z_recv.at[h], device(z_, y, t))
 
     start_step()
     steps = {
@@ -393,7 +399,7 @@
     for name, i in schedule(nz):
         steps[name](i)
 
-    for h in slices:
+    for h in reduce:
         if nz > 1:
             got(recvz.at[pl.ds(0, nz - 1), :, cols[h]], z_recv.at[h])
         v = part[own, :, cols[h]].astype(F32)
@@ -403,7 +409,7 @@
     for ok, whole in line_sent:
         pl.when(ok)(whole)
     for (kind, h), n in counts.items():
-        view = (tok if kind < 3 else part).at[pl.ds(0, n), :, (wide if kind < 3 else cols)[h]]
+        view = (tok if kind < 2 else part).at[pl.ds(0, n), :, (wide, wide, halves, cols)[kind][h]]
         remote(view, view, bulk_send.at[kind, h], z_recv.at[h], partner).wait_send()
 
 
@@ -411,7 +417,7 @@
     rows, width = tokens.shape
     nz, ny, nt = lay.nz, lay.ny, lay.nt
     hidden, shared = wg.shape[2], sg.shape[1]
-    n, most = len(lay.cols), max(nt, ny)
+    n, most = max(GATHER, REDUCE), max(nt, ny)
     many_b = max(1, max((lay.last[h] - 1) * lay.first[h] for h in range(n)) * nz)
     many_a = max(1, (most - 1) * nz)
     vmem = pl.BlockSpec(memory_space=pltpu.VMEM)
@@ -435,16 +441,16 @@
         pltpu.VMEM(su.shape, BF16),
         pltpu.VMEM(sd.shape, BF16),
         dma((9,)),
-        dma((7, n)),
+        dma((4, n)),
         dma((nz + 1,)),
-        dma((n, nz)),
-        dma((n, nz * max(1, most - 1))),
-        dma((n, nz)),
+        dma((GATHER, nz)),
+        dma((GATHER, nz * max(1, most - 1))),
+        dma((GATHER, nz)),
         dma((nz,)),
-        dma((n, nz)),
-        dma((n, 2 * nz)),
-        dma((n, nz)),
-        dma((n,)),
+        dma((2, nz)),
+        dma((REDUCE, nz)),
+        dma((REDUCE, nz)),
+        dma((REDUCE,)),
     ]
     return pl.pallas_call(
         functools.partial(kernel, lay, experts),

time: 48.5 us -> 47.9 us (0.988)
  Pallas kernels: 46.7 us -> 46.1 us
    pallas_call x1, Pallas kernels: 46.7 us -> 46.1 us  [per_device(): pl.pallas_call(functools.partial(kernel, lay, experts), out_shape=jax.Sha...]
where the time goes in v4:
time: 47.9 us; the launch traced here: 47.7 us
  Pallas kernels  46.1 us (96%)
  local copies, waits for them, and re-layouts  1.55 us (3%)
    pallas_call x1, Pallas kernels, per_device(): pl.pallas_call(functools.partial(kernel, lay, experts), out_shape=jax.Sha...  46.1 us
    unnamed x1, local copies, waits for them, and re-layouts  1.55 us

profile of v4, /device:TPU:0, one launch (start us, length us, event | category | flops | bytes accessed | tf_op | source)
XLA Modules:
  0.0 47.7 jit_solution(13605328803203998725)
XLA Ops:
  0.0 46.1 %shard_map.91 = bf16[16,3584]{1,0:T(8,128)(2,1)} custom-call(bf16[16,3584]{1,0:T(8,128)(2,1)} %tok_in.1, s32[8,16]{1,0:T(8,128)} %bitcast.2, f32[8,16]{1,0:T(8,128)} %bitcast.3, bf16[1,3584,512]{2,1,0:T(8,128)(2,1)} %wg_in.1, bf16[1,3584,512]{2,1,0:T(8,128)(2,1)} %wu_in.1, bf16[1,512,3584]{2,1,0:T(8,128)(2,1)} %wd_in.1, bf16[3584,512]{1,0:T(8,128)(2,1)} %sg_in.1, ...), custom_call_target="tpu_custom_call" | custom-call | tf_op jit(solution)/shard_map/pallas_call | solution.py:455
  46.2 1.6 %copy.11 = bf16[16,3584]{1,0:T(8,128)(2,1)} copy(bf16[16,3584]{1,0:T(8,128)(2,1)} %shard_map.91) | data formatting | bytes 229376

commit v5 on v4

--- a/solution.py
+++ b/solution.py
@@ -58,15 +58,17 @@
 
 GATHER = 4
 REDUCE = 4
+CROSS = 2
 
 
 def schedule(nz):
-    ops = ["A2 0", "R 1", "A1m 1", "A1e 1", "R 2", "A1e 2", "R 3", "A1m 2", "A3 0", "A2 1"]
+    ops = ["A2 0", "R 1", "A1m 1", "A1e 1", "R 2", "X 0", "A1e 2", "R 3", "A1m 2"]
     ops += [f"R {i}" for i in range(4, nz)]
-    ops += ["A1m 3", "W 0", "S 0", "U 0"]
+    ops += ["A3 0", "RB 1", "RB 2", "Bm 1", "Be 1", "A2 1", "A1m 3", "W 0", "S 0", "U 0"]
     for i in range(nz):
-        ops += [f"A1m {i + 4}", f"A1e {i + 3}", f"A2 {i + 2}", f"A3 {i + 1}", f"L {i - 1}" if i > 1 else "", f"D {i}"]
-        ops += [f"W {i + 1}", f"A2 {i + 3}", f"U {i + 1}", "L 0"]
+        ops += [f"A1m {i + 4}", f"A1e {i + 3}", f"RB {i + 3}", f"A2 {i + 2}", f"Bm {i + 2}", f"Be {i + 2}", f"Bm {i + 3}" if i + 4 >= nz else ""]
+        ops += [f"A3 {i + 1}", f"L {i - 1}" if i > 1 else "", f"D {i}"]
+        ops += [f"W {i + 1}", f"A2 {i + 3}", f"U {i + 1}", f"Be {i + 3}", "L 0"]
     ops += ["F 1", f"L {nz - 1}"]
     for j in range(2, nz - 1):
         ops += [f"F {j}", f"Z {j - 1}"]
@@ -84,7 +86,7 @@
 
 def kernel(lay, experts, tok_in, ids_in, rw_in, wg_in, wu_in, wd_in, sg_in, su_in, sd_in, out,
            tok, part, ids, rw, recvp, recvb, recva, recvz, hid, hs, wg, wu, wd, sg, su, sd,
-           load_sem, bulk_send, line_send, line_recv, first_recv, last_recv, swap_recv, pair_recv, b_recv, a_recv, z_recv):
+           load_sem, bulk_send, line_send, line_recv, first_recv, last_recv, swap_recv, pair_recv, b_recv, a_recv, z_recv, cross_send, cross_recv):
     nz, ny, nt = lay.nz, lay.ny, lay.nt
     rows, width, chips = lay.rows, lay.width, lay.chips
     e_idx, t, p = lax.axis_index("expert"), lax.axis_index("tensor"), lax.axis_index("pair")
@@ -230,10 +232,84 @@
 
         pl.when(ok)(go)
 
+    crossing = list(gather)[len(gather) - CROSS :]
+    cross_sent = []
+
+    def send_cross(h, slot, z_, target):
+        c = h - crossing[0]
+        ok = (target >= 0) & (target < nz)
+        dev = device(target, y, t)
+
+        def copies():
+            for f in first_peers[h]:
+                view = tok.at[place(p, z_, *yt(h, f, last_at[h])), :, wide[h]]
+                yield remote(view, view, cross_send.at[c, slot], cross_recv.at[c, z_], dev)
+
+        def go():
+            for copy in copies():
+                copy.start()
+
+        def drained():
+            if lay.first[h] > 1:
+                view = tok.at[pl.ds(0, lay.first[h] - 1), :, wide[h]]
+                remote(view, view, cross_send.at[c, slot], cross_recv.at[c, z_], dev).wait_send()
+
+        cross_sent.append((ok, drained))
+        return ok, go
+
+    def start_cross(_):
+        for h in crossing:
+            for slot, target in ((0, z + 1), (nz, z - 1)):
+                ok, start = send_cross(h, slot, z, target)
+                pl.when(ok)(start)
+
+    def take_cross(h, z_):
+        if lay.first[h] > 1:
+            got(tok.at[pl.ds(0, lay.first[h] - 1), :, wide[h]], cross_recv.at[h - crossing[0], z_])
+
+    def relay_cross(k):
+        z_ = hops[k]
+        target, ok = inner(z_)
+        sends = [(h, send_cross(h, k, z_, target)[1]) for h in crossing]
+
+        def go():
+            for h, start in sends:
+                take_cross(h, z_)
+                start()
+
+        pl.when(ok)(go)
+
+    def spread_cross(h, z_):
+        for f in first_peers[h]:
+            blk = place(p, z_, *yt(h, f, last_at[h]))
+            last_sends(h, blk, z_)
+            swap(h, blk, z_)
+
+    def inner_cross(i):
+        def go():
+            for h in crossing:
+                spread_cross(h, seq[i])
+
+        pl.when(inner(seq[i])[1])(go)
+
+    def outer_cross(i):
+        kept = dict(counts)
+
+        def go():
+            for h in crossing:
+                take_cross(h, seq[i])
+                spread_cross(h, seq[i])
+
+        pl.when(jnp.logical_not(inner(seq[i])[1]))(go)
+        counts.clear()
+        counts.update(kept)
+
     def spread(i):
         z_ = seq[i]
         blk = place(p, z_, y, t)
         for h in gather:
+            if i and h in crossing:
+                continue
             for d, v in enumerate(first_peers[h]):
                 send_block(0, h, blk, first_recv.at[h, d * nz + z_], device(z, *yt(h, v, last_at[h])))
         for h in gather:
@@ -265,12 +341,18 @@
         z_ = seq[i]
         for h in gather:
             n = lay.first[h]
+            if i and h in crossing:
+                continue
+            onward = h in crossing
             for d in range(n - 1):
                 f = (first_at[h] + n - 1 - d) % n
                 blk = place(p, z_, *yt(h, f, last_at[h]))
                 got(tok.at[blk, :, wide[h]], first_recv.at[h, d * nz + z_])
-                last_sends(h, blk, z_)
-                swap(h, blk, z_)
+                if not onward:
+                    last_sends(h, blk, z_)
+                    swap(h, blk, z_)
+            if onward:
+                spread_cross(h, z_)
 
     def last_step(i):
         z_ = seq[i]
@@ -393,7 +475,7 @@
 
     start_step()
     steps = {
-        "R": relay_step, "A1m": inner_step, "A1e": outer_step, "A2": first_step, "A3": last_step, "W": partner_wait, "S": shared_up, "U": up, "D": down,
+        "R": relay_step, "X": start_cross, "RB": relay_cross, "Bm": inner_cross, "Be": outer_cross, "A1m": inner_step, "A1e": outer_step, "A2": first_step, "A3": last_step, "W": partner_wait, "S": shared_up, "U": up, "D": down,
         "L": sums_last, "F": sums_first, "Z": sums_line,
     }
     for name, i in schedule(nz):
@@ -406,7 +488,7 @@
         for d in range(nz - 1):
             v = v + recvz[d, :, cols[h]].astype(F32)
         out[:, cols[h]] = v.astype(BF16)
-    for ok, whole in line_sent:
+    for ok, whole in line_sent + cross_sent:
         pl.when(ok)(whole)
     for (kind, h), n in counts.items():
         view = (tok if kind < 2 else part).at[pl.ds(0, n), :, (wide, wide, halves, cols)[kind][h]]
@@ -451,6 +533,8 @@
         dma((REDUCE, nz)),
         dma((REDUCE, nz)),
         dma((REDUCE,)),
+        dma((max(1, CROSS), nz + 1)),
+        dma((max(1, CROSS), nz)),
     ]
     return pl.pallas_call(
         functools.partial(kernel, lay, experts),

time: 47.9 us -> 47.7 us (level)
  no operation moved by 1% of the time
where the time goes in v5:
time: 47.7 us; the launch traced here: 47.5 us
  Pallas kernels  45.9 us (96%)
  local copies, waits for them, and re-layouts  1.55 us (3%)
    pallas_call x1, Pallas kernels, per_device(): pl.pallas_call(functools.partial(kernel, lay, experts), out_shape=jax.Sha...  45.9 us
    unnamed x1, local copies, waits for them, and re-layouts  1.55 us

profile of v5, /device:TPU:0, one launch (start us, length us, event | category | flops | bytes accessed | tf_op | source)
XLA Modules:
  0.0 47.5 jit_solution(9480770405836706220)
XLA Ops:
  0.0 45.9 %shard_map.91 = bf16[16,3584]{1,0:T(8,128)(2,1)} custom-call(bf16[16,3584]{1,0:T(8,128)(2,1)} %tok_in.1, s32[8,16]{1,0:T(8,128)} %bitcast.2, f32[8,16]{1,0:T(8,128)} %bitcast.3, bf16[1,3584,512]{2,1,0:T(8,128)(2,1)} %wg_in.1, bf16[1,3584,512]{2,1,0:T(8,128)(2,1)} %wu_in.1, bf16[1,512,3584]{2,1,0:T(8,128)(2,1)} %wd_in.1, bf16[3584,512]{1,0:T(8,128)(2,1)} %sg_in.1, ...), custom_call_target="tpu_custom_call" | custom-call | tf_op jit(solution)/shard_map/pallas_call | solution.py:539
  45.9 1.6 %copy.11 = bf16[16,3584]{1,0:T(8,128)(2,1)} copy(bf16[16,3584]{1,0:T(8,128)(2,1)} %shard_map.91) | data formatting | bytes 229376

commit v6 on v5

--- a/solution.py
+++ b/solution.py
@@ -86,7 +86,7 @@
 
 def kernel(lay, experts, tok_in, ids_in, rw_in, wg_in, wu_in, wd_in, sg_in, su_in, sd_in, out,
            tok, part, ids, rw, recvp, recvb, recva, recvz, hid, hs, wg, wu, wd, sg, su, sd,
-           load_sem, bulk_send, line_send, line_recv, first_recv, last_recv, swap_recv, pair_recv, b_recv, a_recv, z_recv, cross_send, cross_recv):
+           load_sem, bulk_send, line_send, line_recv, first_recv, last_recv, swap_recv, pair_recv, b_recv, a_recv, z_recv, cross_send, cross_recv, result, store_sem):
     nz, ny, nt = lay.nz, lay.ny, lay.nt
     rows, width, chips = lay.rows, lay.width, lay.chips
     e_idx, t, p = lax.axis_index("expert"), lax.axis_index("tensor"), lax.axis_index("pair")
@@ -106,8 +106,8 @@
     def greet(dev):
         pl.semaphore_signal(barrier, inc=1, device_id=dev, device_id_type=MESH)
 
-    for d in range(1, nz):
-        greet(device((z + d) % nz, y, t))
+    for z_ in (z + 1, z - 1):
+        pl.when((z_ >= 0) & (z_ < nz))(functools.partial(greet, device(z_, y, t)))
     for t_ in t_peers:
         greet(device(z, y, t_))
     for y_ in y_peers:
@@ -164,7 +164,8 @@
     tok[own, :, pl.ds(width, lay.extra)] = turned.astype(BF16)
 
     first.wait()
-    pl.semaphore_wait(barrier, nt + ny + nz - 2)
+    beside = jnp.where(z + 1 < nz, 1, 0) + jnp.where(z > 0, 1, 0)
+    pl.semaphore_wait(barrier, nt + ny - 1 + beside)
 
     def remote(src, dst, sem_send, sem_recv, dev):
         return pltpu.make_async_remote_copy(
@@ -481,18 +482,23 @@
     for name, i in schedule(nz):
         steps[name](i)
 
+    stores = []
     for h in reduce:
         if nz > 1:
             got(recvz.at[pl.ds(0, nz - 1), :, cols[h]], z_recv.at[h])
         v = part[own, :, cols[h]].astype(F32)
         for d in range(nz - 1):
             v = v + recvz[d, :, cols[h]].astype(F32)
-        out[:, cols[h]] = v.astype(BF16)
+        result[:, cols[h]] = v.astype(BF16)
+        stores.append(pltpu.make_async_copy(result.at[:, cols[h]], out.at[:, cols[h]], store_sem.at[h]))
+        stores[-1].start()
     for ok, whole in line_sent + cross_sent:
         pl.when(ok)(whole)
     for (kind, h), n in counts.items():
         view = (tok if kind < 2 else part).at[pl.ds(0, n), :, (wide, wide, halves, cols)[kind][h]]
         remote(view, view, bulk_send.at[kind, h], z_recv.at[h], partner).wait_send()
+    for store in stores:
+        store.wait()
 
 
 def per_device(lay, experts, tokens, ids, rw, wg, wu, wd, sg, su, sd):
@@ -502,7 +508,6 @@
     n, most = max(GATHER, REDUCE), max(nt, ny)
     many_b = max(1, max((lay.last[h] - 1) * lay.first[h] for h in range(n)) * nz)
     many_a = max(1, (most - 1) * nz)
-    vmem = pl.BlockSpec(memory_space=pltpu.VMEM)
     anyw = pl.BlockSpec(memory_space=pl.ANY)
     dma = pltpu.SemaphoreType.DMA
     scratch = [
@@ -535,12 +540,14 @@
         dma((REDUCE,)),
         dma((max(1, CROSS), nz + 1)),
         dma((max(1, CROSS), nz)),
+        pltpu.VMEM((rows, width), BF16),
+        dma((REDUCE,)),
     ]
     return pl.pallas_call(
         functools.partial(kernel, lay, experts),
         out_shape=jax.ShapeDtypeStruct((rows, width), BF16),
         in_specs=[anyw] * 9,
-        out_specs=vmem,
+        out_specs=anyw,
         scratch_shapes=scratch,
         compiler_params=pltpu.CompilerParams(
             collective_id=0, has_side_effects=True, vmem_limit_bytes=67043328

time: 47.7 us -> 47.3 us (level)
  no operation moved by 1% of the time
where the time goes in v6:
time: 47.3 us; the launch traced here: 47.1 us
  Pallas kernels  45.5 us (96%)
  local copies, waits for them, and re-layouts  1.55 us (3%)
    pallas_call x1, Pallas kernels, per_device(): pl.pallas_call(functools.partial(kernel, lay, experts), out_shape=jax.Sha...  45.5 us
    unnamed x1, local copies, waits for them, and re-layouts  1.55 us

profile of v6, /device:TPU:0, one launch (start us, length us, event | category | flops | bytes accessed | tf_op | source)
XLA Modules:
  0.0 47.1 jit_solution(13973624469313695700)
XLA Ops:
  0.0 45.5 %shard_map.91 = bf16[16,3584]{1,0:T(8,128)(2,1)} custom-call(bf16[16,3584]{1,0:T(8,128)(2,1)} %tok_in.1, s32[8,16]{1,0:T(8,128)} %bitcast.2, f32[8,16]{1,0:T(8,128)} %bitcast.3, bf16[1,3584,512]{2,1,0:T(8,128)(2,1)} %wg_in.1, bf16[1,3584,512]{2,1,0:T(8,128)(2,1)} %wu_in.1, bf16[1,512,3584]{2,1,0:T(8,128)(2,1)} %wd_in.1, bf16[3584,512]{1,0:T(8,128)(2,1)} %sg_in.1, ...), custom_call_target="tpu_custom_call" | custom-call | tf_op jit(solution)/shard_map/pallas_call | solution.py:546
  45.5 1.6 %copy.11 = bf16[16,3584]{1,0:T(8,128)(2,1)} copy(bf16[16,3584]{1,0:T(8,128)(2,1)} %shard_map.91) | data formatting | bytes 229376
